TPU v7x, 512 devices: a whole 4x8x8 slice. The times are simulated.
512 devices in a mesh: tm: 64 (over z, y_hi, core), freq: 8 (over y_lo, x).
Axes of the slice: x: 4, y: 8 (y_hi: 4, y_lo: 2; y = y_hi * 2 + y_lo), z: 8, core: 2. Of those that a mesh axis runs over, the one named last changes fastest.
Arguments:
- spec: bfloat16 [256, 8192, 128], P('freq', 'tm')
- segment_ids: int32 [8192], replicated, may hold values from 0 to 63, never falling along the last dimension, each value on 1 to 256 neighbouring positions
- active: int32 [8192], replicated, may hold values 0 or 1
- time_gain: float32 [128], replicated, as said below
- time_match: bfloat16 [128, 128], replicated, may hold values from -0.5 to 0.5
- time_value: bfloat16 [128, 128], replicated, may hold values from -0.5 to 0.5
- time_out: bfloat16 [128, 128], replicated, may hold values from -0.5 to 0.5
- freq_gain: float32 [128], replicated, as said below
- freq_match: bfloat16 [128, 128], replicated, may hold values from -0.5 to 0.5
- freq_value: bfloat16 [128, 128], replicated, may hold values from -0.5 to 0.5
- freq_out: bfloat16 [128, 128], replicated, may hold values from -0.5 to 0.5
- mlp_gain: float32 [128], replicated, may hold values from 0.1 to 1.9
- mlp_up: bfloat16 [128, 512], replicated, may hold values from -0.5 to 0.5
- mlp_down: bfloat16 [512, 128], replicated, may hold values from -0.25 to 0.25
Outputs:
- block_out: bfloat16 [256, 8192, 128], P('freq', 'tm')
Inputs may be any that keep to these rules, and one draw needn't show every extreme that they name: `segment_ids`: never falling along the frames; each recording spans 1 to 256 frames, one exactly that many. `time_gain`: positive. `freq_gain`: positive.
All inputs are finite; a program needn't handle non-finite values.
Results may differ from a plain program's by a relative error of at most 0.017.
The roundings to bfloat16 on the way count: a program that leaves them out, or rounds other values in their place, can miss the bound.
Values may be sent and summed in bfloat16 or wider, within the bound.
No kernel may reach another device: no remote copies, remote signals or barrier semaphores. Data moves between devices by JAX's collectives and lax.ppermute only.
A program may use at most 64 MiB of HBM per device.

v0:
```python
import math

import jax
import jax.numpy as jnp
from jax import lax
from jax.sharding import PartitionSpec as P

HEADS = 4
HALO = 64


def with_halo(array, sides, width):
    for axis, dim in sides:
        peers, length = (lax.axis_size(axis), array.shape[dim])
        up = [(i, (i + 1) % peers) for i in range(peers - 1)]
        down = [(j, i) for i, j in up]
        last = lax.slice_in_dim(array, length - width, length, axis=dim)
        initial = lax.slice_in_dim(array, 0, width, axis=dim)
        before = lax.ppermute(last, axis, up)
        after = lax.ppermute(initial, axis, down)
        array = jnp.concatenate([before, array, after], axis=dim)
    return array


def layer_norm(values, gain):
    widened = values.astype(jnp.float32)
    centred = widened - jnp.mean(widened, -1, keepdims=True)
    spread = jnp.mean(centred * centred, -1, keepdims=True)
    return (centred * lax.rsqrt(spread + 1e-05) * gain).astype(jnp.bfloat16)


def project(values, weight):
    return jnp.dot(values, weight, preferred_element_type=jnp.float32).astype(jnp.bfloat16)


def add_branch(base, mixed, weight):
    return (
        base.astype(jnp.float32) + jnp.dot(mixed, weight, preferred_element_type=jnp.float32)
    ).astype(jnp.bfloat16)


def attend(query, key_rows, value_rows, allowed):
    heads_q = query.reshape(query.shape[:-1] + (HEADS, -1))
    heads_k = key_rows.reshape(key_rows.shape[:-1] + (HEADS, -1))
    heads_v = value_rows.reshape(value_rows.shape[:-1] + (HEADS, -1))
    scores = jnp.einsum(
        "...thd,...shd->...hts", heads_q, heads_k, preferred_element_type=jnp.float32
    ) * heads_q.shape[-1] ** (-0.5)
    if allowed is not None:
        scores = jnp.where(allowed, scores, -1e30)
    largest = jnp.max(scores, -1, keepdims=True)
    weights = jnp.exp(scores - largest)
    shares = (weights / jnp.sum(weights, -1, keepdims=True)).astype(jnp.bfloat16)
    mixed = jnp.einsum("...hts,...shd->...thd", shares, heads_v, preferred_element_type=jnp.float32)
    return mixed.reshape(query.shape).astype(jnp.bfloat16)


def freq_attend(normed, weight_match, weight_value):
    match_rows = project(normed, weight_match)
    value_rows = project(normed, weight_value)
    bins, count, width = match_rows.shape
    group = math.gcd(count, 2)
    match_frames = jnp.moveaxis(match_rows, 1, 0).reshape(count // group, group, bins, width)
    value_frames = jnp.moveaxis(value_rows, 1, 0).reshape(count // group, group, bins, width)

    def one_group(items):
        return attend(items[0], items[0], items[1], None)

    mixed = lax.map(one_group, (match_frames, value_frames)).reshape(count, bins, width)
    return jnp.moveaxis(mixed, 0, 1)


def feed_forward(after_freq, mlp_gain, mlp_up, mlp_down):
    hidden = jax.nn.gelu(
        jnp.dot(layer_norm(after_freq, mlp_gain), mlp_up, preferred_element_type=jnp.float32)
    ).astype(jnp.bfloat16)
    return add_branch(after_freq, hidden, mlp_down)


def per_device(
    spec,
    segment_ids,
    active,
    time_gain,
    time_match,
    time_value,
    time_out,
    freq_gain,
    freq_match,
    freq_value,
    freq_out,
    mlp_gain,
    mlp_up,
    mlp_down,
):
    bins_dev, frames_dev, width = spec.shape
    frames = segment_ids.shape[0]
    span = frames_dev + 2 * HALO
    start = lax.axis_index("tm") * frames_dev
    normed = layer_norm(spec, time_gain)
    match_rows = project(normed, time_match)
    value_rows = project(normed, time_value)
    stacked = jnp.concatenate([match_rows, value_rows], 2)
    widened = with_halo(stacked, (("tm", 1),), HALO)
    key_rows = widened[:, :, :width]
    key_values = widened[:, :, width:]
    pad_segment = jnp.pad(segment_ids, HALO, constant_values=-1)
    pad_active = jnp.pad(active, HALO)
    seg_query = lax.dynamic_slice_in_dim(segment_ids, start, frames_dev, 0)
    seg_key = lax.dynamic_slice_in_dim(pad_segment, start, span, 0)
    act_key = lax.dynamic_slice_in_dim(pad_active, start, span, 0)
    pos_query = start + jnp.arange(frames_dev, dtype=jnp.int32)
    pos_key = start - HALO + jnp.arange(span, dtype=jnp.int32)
    inside = (pos_key >= 0) & (pos_key < frames)
    allowed = (
        inside[None, :]
        & (seg_query[:, None] == seg_key[None, :])
        & ((act_key[None, :] == 1) | (pos_query[:, None] == pos_key[None, :]))
    )
    group = math.gcd(bins_dev, 2)

    def time_group(items):
        return attend(items[0], items[1], items[2], allowed)

    time_mix = lax.map(
        time_group,
        (
            match_rows.reshape(bins_dev // group, group, frames_dev, width),
            key_rows.reshape(bins_dev // group, group, span, width),
            key_values.reshape(bins_dev // group, group, span, width),
        ),
    )
    time_mix = time_mix.reshape(bins_dev, frames_dev, width)
    after_time = add_branch(spec, time_mix, time_out)
    freq_normed = layer_norm(after_time, freq_gain)
    full_bins = lax.all_to_all(freq_normed, "freq", split_axis=1, concat_axis=0, tiled=True)
    mixed_full = freq_attend(full_bins, freq_match, freq_value)
    freq_mix = lax.all_to_all(mixed_full, "freq", split_axis=0, concat_axis=1, tiled=True)
    after_freq = add_branch(after_time, freq_mix, freq_out)
    return feed_forward(after_freq, mlp_gain, mlp_up, mlp_down)


def solution(mesh):
    placed = (
        P("freq", "tm", None),
        P(),
        P(),
        P(),
        P(),
        P(),
        P(),
        P(),
        P(),
        P(),
        P(),
        P(),
        P(),
        P(),
    )
    return jax.shard_map(
        per_device, mesh=mesh, in_specs=placed, out_specs=P("freq", "tm", None), check_vma=False
    )
```

profile of v0, /device:TPU:448, one launch (start us, length us, event | category | flops | bytes accessed | tf_op | source)
XLA Modules:
  0.0 225.3 jit_solution(6609730374367023469)
XLA Ops:
  0.0 1.7 copy.49
  3.4 2.2 slice_maximum_fusion
  5.6 2.7 %copy.54 = bf16[32,64,256]{2,1,0:T(8,128)(2,1)} copy(bf16[32,64,256]{1,2,0:T(8,128)(2,1)} %get-tuple-element.139) | data formatting | bytes 2097152 | tf_op jit(solution)/shard_map/slice | solution.py:17
  8.3 2.0 collective-permute-start
  10.4 1.6 copy.55
  12.0 6.6 %collective-permute-start.1 = (bf16[32,64,256]{2,1,0:T(8,128)(2,1)}, bf16[32,64,256]{2,1,0:T(8,128)(2,1)}, u32[]{:S(2)}, u32[]{:S(2)}) collective-permute-start(bf16[32,64,256]{2,1,0:T(8,128)(2,1)} %copy.55), channel_id=1, source_target_pairs={{8,0},{16,8},{24,16},{32,24},{40,32},{48,40},{56,48},{64,56},{72,6... | collective-permute-start | bytes 3145736 | tf_op jit(solution)/shard_map/ppermute | solution.py:20
  18.9 15.9 %collective-permute-done = bf16[32,64,256]{2,1,0:T(8,128)(2,1)} collective-permute-done((bf16[32,64,256]{2,1,0:T(8,128)(2,1)}, bf16[32,64,256]{2,1,0:T(8,128)(2,1)}, u32[]{:S(2)}, u32[]{:S(2)}) %collective-permute-start) | collective-permute-done | bytes 1048608 | tf_op jit(solution)/shard_map/ppermute | solution.py:19
  34.8 2.0 copy.56
  36.8 5.6 %collective-permute-done.1 = bf16[32,64,256]{2,1,0:T(8,128)(2,1)} collective-permute-done((bf16[32,64,256]{2,1,0:T(8,128)(2,1)}, bf16[32,64,256]{2,1,0:T(8,128)(2,1)}, u32[]{:S(2)}, u32[]{:S(2)}) %collective-permute-start.1) | collective-permute-done | bytes 1048608 | tf_op jit(solution)/shard_map/ppermute | solution.py:20
  42.5 2.8 %copy.57 = bf16[32,64,256]{1,2,0:T(8,128)(2,1)} copy(bf16[32,64,256]{2,1,0:T(8,128)(2,1)} %collective-permute-done.1) | data formatting | bytes 2097152 | tf_op jit(solution)/shard_map/ppermute | solution.py:20
  45.3 4.8 %pad_maximum_fusion = bf16[32,256,256]{1,2,0:T(8,128)(2,1)S(1)} fusion(bf16[32,64,256]{1,2,0:T(8,128)(2,1)} %copy.57, bf16[32,128,128]{1,2,0:T(8,128)(2,1)} %copy-done.2, bf16[32,128,128]{1,2,0:T(8,128)(2,1)} %copy-done.1, bf16[32,64,256]{1,2,0:T(8,128)(2,1)S(1)} %copy.56), kind=kLoop, calls=%fused_computation.39 | loop fusion | flops 16777216 | bytes 8388608 | tf_op jit(solution)/shard_map/concatenate | solution.py:21
  50.0 2.4 %fusion.80 = (bf16[32,256,128]{1,2,0:T(8,128)(2,1)}, bf16[32,256,128]{1,2,0:T(8,128)(2,1)}) fusion(bf16[32,256,256]{1,2,0:T(8,128)(2,1)S(1)} %pad_maximum_fusion), kind=kLoop, calls=%fused_computation.104 | loop fusion | bytes 8388608 | tf_op jit(solution)/shard_map/slice | solution.py:105
  52.5 88.3 %while.22 = (s32[]{:T(128)}, bf16[16,2,128,128]{2,3,1,0:T(8,128)(2,1)}, bf16[16,2,256,128]{2,3,1,0:T(8,128)(2,1)}, bf16[16,2,128,128]{2,3,1,0:T(8,128)(2,1)}, bf...) while((s32[]{:T(128)}, ...), condition=%wide.region_5.6_spmd.clone, body=%wide.region_2.5_spmd.clone.sunk | while | flops 52889088 | bytes 3584125 | solution.py:125
  52.5 1.0 constant_dynamic-slice_fusion.9
  55.4 1.9 convolution_convert_fusion.9
  58.0 1.0 constant_dynamic-slice_fusion.9
  60.9 1.9 convolution_convert_fusion.9
  66.5 1.9 convolution_convert_fusion.9
  72.0 1.9 convolution_convert_fusion.9
  77.5 1.9 convolution_convert_fusion.9
  83.0 1.9 convolution_convert_fusion.9
  88.5 1.9 convolution_convert_fusion.9
  94.0 1.9 convolution_convert_fusion.9
  99.6 1.9 convolution_convert_fusion.9
  105.1 1.9 convolution_convert_fusion.9
  110.6 1.9 convolution_convert_fusion.9
  116.1 1.9 convolution_convert_fusion.9
  121.6 1.9 convolution_convert_fusion.9
  127.1 1.9 convolution_convert_fusion.9
  132.6 1.9 convolution_convert_fusion.9
  138.2 1.9 convolution_convert_fusion.9
  140.7 1.8 convert_reduce_fusion.1
  143.4 1.7 copy.60
  145.1 4.4 %all-to-all-start = ((bf16[32,128,128]{2,0,1:T(8,128)(2,1)}), bf16[32,128,128]{2,0,1:T(8,128)(2,1)S(1)}, u32[]{:S(2)}, u32[]{:S(2)}) async-start(bf16[32,128,128]{2,0,1:T(8,128)(2,1)} %copy.60), calls=%async_computation | async-start | bytes 2097152 | tf_op jit(solution)/shard_map/all_to_all | solution.py:136
  149.5 15.8 %all-to-all-done = bf16[32,128,128]{2,0,1:T(8,128)(2,1)S(1)} async-done(((bf16[32,128,128]{2,0,1:T(8,128)(2,1)}), bf16[32,128,128]{2,0,1:T(8,128)(2,1)S(1)}, u32[]{:S(2)}, u32[]{:S(2)}) %all-to-all-start) | async-done | bytes 1048608 | tf_op jit(solution)/shard_map/all_to_all | solution.py:136
  166.1 1.4 convolution_convert_fusion.2
  167.5 31.8 %while.21 = (s32[]{:T(128)}, bf16[8,2,256,128]{3,1,0,2:T(2,128)(2,1)}, bf16[8,2,256,128]{3,2,1,0:T(8,128)(2,1)S(1)}, bf16[8,2,256,128]{3,2,1,0:T(8,128)(2,1)}, s32[]{:T(128)}) while((s32[]{:T(128)}, bf16[8,2,256,128]{3,1,0,2:T(2,128)(2,1)}, bf16[8,2,256,128]{3,2,1,0:T(8,128)(2,1)S(1)}, bf16[8,2,256,128]{3,2,1,0:T(8,128)(2,1)}, ...), condition=%wide.region_11.12_spmd, body=%wide.region_8.11_spmd.sunk | while | flops 104401408 | bytes 2114113 | solution.py:69
  169.6 1.1 convolution_convert_fusion.8
  173.5 1.1 convolution_convert_fusion.8
  177.5 1.1 convolution_convert_fusion.8
  181.5 1.1 convolution_convert_fusion.8
  185.5 1.1 convolution_convert_fusion.8
  189.4 1.1 convolution_convert_fusion.8
  193.4 1.1 convolution_convert_fusion.8
  197.4 1.1 convolution_convert_fusion.8
  199.3 19.8 %all_to_all.36 = bf16[256,16,128]{2,1,0:T(8,128)(2,1)S(1)} all-to-all(bf16[256,16,128]{2,1,0:T(8,128)(2,1)} %bitcast.131), channel_id=1, replica_groups=mesh['tm'=64,'freq'=8] {'freq'}, dimensions={0} | all-to-all | bytes 2097152 | tf_op jit(solution)/shard_map/all_to_all | solution.py:138
  220.4 3.6 %fusion.51 = bf16[32,128,128]{1,2,0:T(8,128)(2,1)S(1)} fusion(bf16[32,128,128]{1,2,0:T(8,128)(2,1)S(1)} %get-tuple-element.144, f32[128]{0:T(128)S(1)} %copy-done.14, f32[32,128]{1,0:T(8,128)S(1)} %add_rsqrt_fusion, f32[32,128]{1,0:T(8,128)S(1)} %broadcast_multiply_fusion, bf16[512,128]{1,0:T(8,128)(2,1)S(1)} %copy-done, bf16[128,512]{1,0:T(8,128)(2,1)S(1)} %copy-done.10), kind=kOutput, calls=%fused_computation.68 | convolution fusion | flops 1096810496 | bytes 2392576 | tf_op jit(solution)/shard_map/dot_general | solution.py:38
  224.0 1.3 copy.70
  (195 shorter events, 83.3 us)
Async XLA Ops:
  0.0 220.3 %copy-start = (bf16[512,128]{1,0:T(8,128)(2,1)S(1)}, bf16[512,128]{1,0:T(8,128)(2,1)}, u32[]{:S(2)}) copy-start(bf16[512,128]{1,0:T(8,128)(2,1)} %param.31) | copy-start | bytes 393220
  0.0 2.2 copy-start.13
  0.0 2.3 %copy-start.11 = (bf16[128,128]{1,0:T(8,128)(2,1)S(1)}, bf16[128,128]{1,0:T(8,128)(2,1)}, u32[]{:S(2)}) copy-start(bf16[128,128]{1,0:T(8,128)(2,1)} %param.22) | copy-start | bytes 98308
  1.7 1.1 copy-start.12
  2.8 2.8 %copy-start.1 = (bf16[32,128,128]{1,2,0:T(8,128)(2,1)}, bf16[32,128,128]{1,2,0:T(8,128)(2,1)S(1)}, u32[]{:S(2)}) copy-start(bf16[32,128,128]{1,2,0:T(8,128)(2,1)S(1)} %convolution_convert_fusion.5) | copy-start | bytes 3145732
  3.4 2.2 copy-start.2
  8.3 10.4 %copy-start.8 = (s32[8192]{0:T(1024)S(1)}, s32[8192]{0:T(1024)}, u32[]{:S(2)}) copy-start(s32[8192]{0:T(1024)} %param.19) | copy-start | bytes 98308
  8.3 10.4 %copy-start.7 = (s32[8192]{0:T(1024)S(1)}, s32[8192]{0:T(1024)}, u32[]{:S(2)}) copy-start(s32[8192]{0:T(1024)} %param.20) | copy-start | bytes 98308
  8.3 26.5 %collective-permute-start = (bf16[32,64,256]{2,1,0:T(8,128)(2,1)}, bf16[32,64,256]{2,1,0:T(8,128)(2,1)}, u32[]{:S(2)}, u32[]{:S(2)}) collective-permute-start(bf16[32,64,256]{2,1,0:T(8,128)(2,1)} %copy.54), channel_id=1, source_target_pairs={{0,8},{8,16},{16,24},{24,32},{32,40},{40,48},{48,56},{56,64},{64,7... | collective-permute-start | bytes 3145736 | tf_op jit(solution)/shard_map/ppermute | solution.py:19
  12.0 30.5 %collective-permute-start.1 = (bf16[32,64,256]{2,1,0:T(8,128)(2,1)}, bf16[32,64,256]{2,1,0:T(8,128)(2,1)}, u32[]{:S(2)}, u32[]{:S(2)}) collective-permute-start(bf16[32,64,256]{2,1,0:T(8,128)(2,1)} %copy.55), channel_id=1, source_target_pairs={{8,0},{16,8},{24,16},{32,24},{40,32},{48,40},{56,48},{64,56},{72,6... | collective-permute-start | bytes 3145736 | tf_op jit(solution)/shard_map/ppermute | solution.py:20
  52.5 88.3 %copy-start.3 = (bf16[128,128]{1,0:T(8,128)(2,1)S(1)}, bf16[128,128]{1,0:T(8,128)(2,1)}, u32[]{:S(2)}) copy-start(bf16[128,128]{1,0:T(8,128)(2,1)} %param.24) | copy-start | bytes 98308
  140.7 2.2 copy-start.9
  145.1 20.4 %copy-start.4 = (bf16[128,128]{1,0:T(8,128)(2,1)S(1)}, bf16[128,128]{1,0:T(8,128)(2,1)}, u32[]{:S(2)}) copy-start(bf16[128,128]{1,0:T(8,128)(2,1)} %param.27) | copy-start | bytes 98308
  145.1 20.3 %all-to-all-start = ((bf16[32,128,128]{2,0,1:T(8,128)(2,1)}), bf16[32,128,128]{2,0,1:T(8,128)(2,1)S(1)}, u32[]{:S(2)}, u32[]{:S(2)}) async-start(bf16[32,128,128]{2,0,1:T(8,128)(2,1)} %copy.60), calls=%async_computation | async-start | bytes 2097152 | tf_op jit(solution)/shard_map/all_to_all | solution.py:136
  165.4 0.8 copy-start.5
  199.3 20.1 %copy-start.6 = (bf16[128,128]{1,0:T(8,128)(2,1)S(1)}, bf16[128,128]{1,0:T(8,128)(2,1)}, u32[]{:S(2)}) copy-start(bf16[128,128]{1,0:T(8,128)(2,1)} %param.28) | copy-start | bytes 98308
  219.4 1.0 copy-start.10
  219.4 1.0 copy-start.14
where the time goes:
time: 227 us; the launch traced here: 225 us
  local copies, waits for them, and re-layouts  73.1 us (32%)
  matrix products  70.4 us (31%)
  waiting for transfers between devices  37.4 us (16%)
  blocking collectives  19.8 us (9%)
  starting transfers between devices  13.1 us (6%)
  other arithmetic  10.6 us (5%)
    dot_general x24, matrix products, attend(): jnp.einsum('...hts,...shd->...thd', shares, heads_v, preferred_element_ty...  38.9 us
    dynamic_slice x32, local copies, waits for them, and re-layouts, per_device(): lax.map(time_group, (match_rows.reshape(bins_dev // group, group, frames_...  29.4 us
    all_to_all x1, blocking collectives, per_device(): lax.all_to_all(mixed_full, 'freq', split_axis=0, concat_axis=1, tiled=True)  19.8 us
    sub x24, matrix products, attend(): weights = jnp.exp(scores - largest)  17.1 us
    ppermute x1, waiting for transfers between devices, with_halo(): before = lax.ppermute(last, axis, up)  15.9 us
    all_to_all x1, waiting for transfers between devices, per_device(): lax.all_to_all(freq_normed, 'freq', split_axis=1, concat_axis=0, tiled=True)  15.8 us
    dynamic_update_slice x16, local copies, waits for them, and re-layouts, per_device(): lax.map(time_group, (match_rows.reshape(bins_dev // group, group, frames_...  10.5 us
    dynamic_slice x24, local copies, waits for them, and re-layouts, freq_attend(): lax.map(one_group, (match_frames, value_frames)).reshape(count, bins, width)  9.23 us
  transfers between devices with their start and end apart: 3, of which 3 were waited for; matrix products, arithmetic and copies ran while one was open for 2% of the time, Pallas kernels for 0%

commit v1 on v0

v1 whole, which is shorter than its diff:
```python
import functools
import math

import jax
import jax.numpy as jnp
from jax import lax
from jax.experimental import pallas as pl
from jax.experimental.pallas import tpu as pltpu
from jax.sharding import PartitionSpec as P

HEADS = 4
HALO = 64
GROUP = 16
F32 = jnp.float32
BF16 = jnp.bfloat16
NEG = -1e30
ONES_ROWS = 16


def layer_norm(values, gain):
    widened = values.astype(F32)
    centred = widened - jnp.mean(widened, -1, keepdims=True)
    spread = jnp.mean(centred * centred, -1, keepdims=True)
    return (centred * lax.rsqrt(spread + 1e-05) * gain).astype(BF16)


def dot_nt(a, b):
    return lax.dot_general(a, b, (((1,), (1,)), ((), ())), preferred_element_type=F32)


def dot_tn(a, b):
    return lax.dot_general(a, b, (((0,), (0,)), ((), ())), preferred_element_type=F32)


def dot_nn(a, b):
    return jnp.dot(a, b, preferred_element_type=F32)


def head_scales(width):
    head = lax.broadcasted_iota(jnp.int32, (1, width), 1) // (width // HEADS)
    scale = (width // HEADS) ** (-0.5) * math.log2(math.e)
    return [jnp.where(head == h, scale, 0.0).astype(F32) for h in range(HEADS)]


def mix_heads(key_rows, query, values_t, scales, key_extra, query_extra):
    count = query.shape[0]
    width = query.shape[1] // HEADS
    wide = query.astype(F32)
    pieces = []
    for h in range(HEADS):
        side = (wide * scales[h]).astype(BF16)
        if query_extra is not None:
            side = jnp.concatenate([side, query_extra], 1)
        rows = key_rows if key_extra is None else jnp.concatenate([key_rows, key_extra], 1)
        scores = dot_nt(rows, side)
        weights = jnp.exp2(scores - jnp.max(scores, 0, keepdims=True)).astype(BF16)
        own = jnp.concatenate(
            [values_t[h * width : (h + 1) * width], jnp.ones((ONES_ROWS, values_t.shape[1]), BF16)], 0
        )
        mixed = dot_nn(own, weights)
        pieces.append(mixed[:width] / mixed[width : width + 1])
    return jnp.concatenate(pieces, 0)


def time_kernel(before, own, after, bias, eye, time_gain, match, value_t, out_w, freq_gain, after_time, sent, turned):
    scales = head_scales(own.shape[2])
    count = own.shape[1]

    def one_bin(b, carry):
        spec = own[b]
        joined = jnp.concatenate([before[b], spec, after[b]], 0)
        normed = layer_norm(joined, time_gain[...])
        key_rows = dot_nn(normed, match[...]).astype(BF16)
        values_t = dot_nt(value_t[...], normed).astype(BF16)
        mixed = mix_heads(key_rows, key_rows[HALO : HALO + count], values_t, scales, bias[...], eye[...])
        result = (spec.astype(F32) + dot_tn(mixed.astype(BF16), out_w[...])).astype(BF16)
        after_time[b] = result
        turned[pl.ds(b, count, stride=GROUP), :] = layer_norm(result, freq_gain[...]).astype(F32)
        return carry

    lax.fori_loop(0, GROUP, one_bin, 0, unroll=2)
    sent[...] = turned[...].reshape(count, GROUP, own.shape[2]).astype(BF16)


def freq_kernel(rows, match, value_t, mixed_out):
    parts, frames, each, width = rows.shape
    scales = head_scales(width)

    def one_frame(f, carry):
        normed = rows[:, f].reshape(parts * each, width)
        key_rows = dot_nn(normed, match[...]).astype(BF16)
        values_t = dot_nt(value_t[...], normed).astype(BF16)
        mixed = mix_heads(key_rows, key_rows, values_t, scales, None, None)
        mixed_out[:, f] = mixed.T.astype(BF16).reshape(parts, each, width)
        return carry

    lax.fori_loop(0, frames, one_frame, 0, unroll=1)


def mlp_kernel(mixed, after_time, out_w, gain, up, down, block_out, turned):
    count, group, width = mixed.shape
    turned[...] = mixed[...].astype(F32).reshape(count * group, width)

    def one_bin(b, carry):
        mix = turned[pl.ds(b, count, stride=group), :].astype(BF16)
        after_freq = (after_time[b].astype(F32) + dot_nn(mix, out_w[...])).astype(BF16)
        hidden = jax.nn.gelu(dot_nn(layer_norm(after_freq, gain[...]), up[...])).astype(BF16)
        block_out[b] = (after_freq.astype(F32) + dot_nn(hidden, down[...])).astype(BF16)
        return carry

    lax.fori_loop(0, group, one_bin, 0, unroll=2)


def full(array):
    return pl.BlockSpec(array.shape, lambda i: (0,) * array.ndim)


def params():
    return pltpu.CompilerParams(dimension_semantics=("arbitrary",), vmem_limit_bytes=48 << 20)


def time_stage(before, spec, after, bias, eye, time_gain, match, value_t, out_w, freq_gain):
    bins, count, width = spec.shape
    bin_block = lambda n: pl.BlockSpec((GROUP, n, width), lambda i: (i, 0, 0))
    return pl.pallas_call(
        time_kernel,
        grid=(bins // GROUP,),
        in_specs=[bin_block(HALO), bin_block(count), bin_block(HALO)]
        + [full(a) for a in (bias, eye, time_gain, match, value_t, out_w, freq_gain)],
        out_specs=[bin_block(count), pl.BlockSpec((count, GROUP, width), lambda i: (0, i, 0))],
        out_shape=[
            jax.ShapeDtypeStruct((bins, count, width), BF16),
            jax.ShapeDtypeStruct((count, bins, width), BF16),
        ],
        scratch_shapes=[pltpu.VMEM((count * GROUP, width), F32)],
        compiler_params=params(),
        name="time_stage",
    )(before, spec, after, bias, eye, time_gain, match, value_t, out_w, freq_gain)


def freq_stage(rows, match, value_t, step):
    parts, frames, each, width = rows.shape
    block = pl.BlockSpec((parts, step, each, width), lambda i: (0, i, 0, 0))
    return pl.pallas_call(
        freq_kernel,
        grid=(frames // step,),
        in_specs=[block, full(match), full(value_t)],
        out_specs=block,
        out_shape=jax.ShapeDtypeStruct(rows.shape, BF16),
        compiler_params=params(),
        name="freq_stage",
    )(rows, match, value_t)


def mlp_stage(mixed, after_time, out_w, gain, up, down):
    bins, count, width = after_time.shape
    return pl.pallas_call(
        mlp_kernel,
        grid=(bins // GROUP,),
        in_specs=[
            pl.BlockSpec((count, GROUP, width), lambda i: (0, i, 0)),
            pl.BlockSpec((GROUP, count, width), lambda i: (i, 0, 0)),
        ]
        + [full(a) for a in (out_w, gain, up, down)],
        out_specs=pl.BlockSpec((GROUP, count, width), lambda i: (i, 0, 0)),
        out_shape=jax.ShapeDtypeStruct((bins, count, width), BF16),
        scratch_shapes=[pltpu.VMEM((count * GROUP, width), F32)],
        compiler_params=params(),
        name="mlp_stage",
    )(mixed, after_time, out_w, gain, up, down)


def key_bias(segment_ids, active, count):
    frames = segment_ids.shape[0]
    span = count + 2 * HALO
    start = lax.axis_index("tm") * count
    seg_query = lax.dynamic_slice_in_dim(segment_ids, start, count, 0)
    seg_key = lax.dynamic_slice_in_dim(jnp.pad(segment_ids, HALO, constant_values=-1), start, span, 0)
    act_key = lax.dynamic_slice_in_dim(jnp.pad(active, HALO), start, span, 0)
    pos_key = start - HALO + jnp.arange(span, dtype=jnp.int32)
    pos_query = start + jnp.arange(count, dtype=jnp.int32)
    inside = (pos_key >= 0) & (pos_key < frames)
    allowed = (
        inside[:, None]
        & (seg_query[None, :] == seg_key[:, None])
        & ((act_key[:, None] == 1) | (pos_query[None, :] == pos_key[:, None]))
    )
    return jnp.where(allowed, 0.0, NEG).astype(BF16)


def per_device(
    spec,
    segment_ids,
    active,
    time_gain,
    time_match,
    time_value,
    time_out,
    freq_gain,
    freq_match,
    freq_value,
    freq_out,
    mlp_gain,
    mlp_up,
    mlp_down,
):
    bins, count, width = spec.shape
    peers = lax.axis_size("tm")
    split = lax.axis_size("freq")
    up = [(i, i + 1) for i in range(peers - 1)]
    down = [(j, i) for i, j in up]
    before = lax.ppermute(spec[:, count - HALO :], "tm", up)
    after = lax.ppermute(spec[:, :HALO], "tm", down)
    bias = key_bias(segment_ids, active, count)
    after_time, sent = time_stage(
        before,
        spec,
        after,
        bias,
        jnp.eye(count, dtype=BF16),
        time_gain[None],
        time_match,
        time_value.T,
        time_out,
        freq_gain[None],
    )
    gathered = lax.all_to_all(sent, "freq", split_axis=0, concat_axis=0, tiled=True)
    mixed = freq_stage(
        gathered.reshape(split, count // split, bins, width), freq_match, freq_value.T, 4
    )
    returned = lax.all_to_all(
        mixed.reshape(count, bins, width), "freq", split_axis=0, concat_axis=0, tiled=True
    )
    return mlp_stage(returned, after_time, freq_out, mlp_gain[None], mlp_up, mlp_down)


def solution(mesh):
    placed = (P("freq", "tm", None),) + (P(),) * 13
    return jax.shard_map(
        per_device, mesh=mesh, in_specs=placed, out_specs=P("freq", "tm", None), check_vma=False
    )
```

time: 227 us -> 160 us (0.70)
  Pallas kernels: 0 us -> 96.4 us
  matrix products: 70.4 us -> 0 us
  local copies, waits for them, and re-layouts: 73.1 us -> 3.65 us
  waiting for transfers between devices: 37.4 us -> 26.7 us
  other arithmetic: 10.6 us -> 0.38 us
    pallas_call x0 -> x3, Pallas kernels: none -> 96.4 us  [the longest x1 52.5 us: time_stage(): pl.pallas_call(time_kernel, grid=(bins // GROUP,), in_specs=[bin_block(HA...]
    dot_general x47 -> x0, matrix products: 53.3 us -> none  [the longest x24 38.9 us: attend(): jnp.einsum('...hts,...shd->...thd', shares, heads_v, preferred_element_ty...]
    dynamic_slice x57 -> x1, local copies, waits for them, and re-layouts: 38.7 us -> 0.07 us  [key_bias(): seg_query = lax.dynamic_slice_in_dim(segment_ids, start, count, 0)]
    dynamic_update_slice x32 -> x0, local copies, waits for them, and re-layouts: 17.5 us -> none  [the longest x16 10.5 us: per_device(): lax.map(time_group, (match_rows.reshape(bins_dev // group, group, frames_...]
    sub x24 -> x0, matrix products: 17.1 us -> none  [attend(): weights = jnp.exp(scores - largest)]
    ppermute x2, waiting for transfers between devices: 21.5 us -> 11 us  [the longest x1 6.39 us: per_device(): before = lax.ppermute(spec[:, count - HALO:], 'tm', up)]
    concatenate x2 -> x0, other arithmetic: 6.97 us -> none  [the longest x1 4.76 us: with_halo(): array = jnp.concatenate([before, array, after], axis=dim)]
    slice x3 -> x1, local copies, waits for them, and re-layouts: 6.75 us -> 1.37 us  [per_device(): after = lax.ppermute(spec[:, :HALO], 'tm', down)]
  transfers between devices with their start and end apart: 3 -> 3, of which waited for: 3 -> 3; matrix products, arithmetic and copies ran while one was open for 2% -> 0% of each run, Pallas kernels for 0% -> 0%
where the time goes in v1:
time: 160 us
  Pallas kernels  96.4 us (60%)
  waiting for transfers between devices  26.7 us (17%)
  blocking collectives  19.5 us (12%)
  starting transfers between devices  13 us (8%)
  local copies, waits for them, and re-layouts  3.65 us (2%)
    pallas_call x1, Pallas kernels, time_stage(): pl.pallas_call(time_kernel, grid=(bins // GROUP,), in_specs=[bin_block(HA...  52.5 us
    pallas_call x1, Pallas kernels, freq_stage(): pl.pallas_call(freq_kernel, grid=(frames // step,), in_specs=[block, full...  24.3 us
    pallas_call x1, Pallas kernels, mlp_stage(): pl.pallas_call(mlp_kernel, grid=(bins // GROUP,), in_specs=[pl.BlockSpec(...  19.6 us
    all_to_all x1, blocking collectives, per_device(): lax.all_to_all(mixed.reshape(count, bins, width), 'freq', split_axis=0, c...  19.5 us
    all_to_all x1, waiting for transfers between devices, per_device(): lax.all_to_all(sent, 'freq', split_axis=0, concat_axis=0, tiled=True)  15.6 us
    ppermute x1, starting transfers between devices, per_device(): after = lax.ppermute(spec[:, :HALO], 'tm', down)  6.65 us
    ppermute x1, waiting for transfers between devices, per_device(): before = lax.ppermute(spec[:, count - HALO:], 'tm', up)  6.39 us
    ppermute x1, waiting for transfers between devices, per_device(): after = lax.ppermute(spec[:, :HALO], 'tm', down)  4.63 us
  transfers between devices with their start and end apart: 3, of which 3 were waited for; matrix products, arithmetic and copies ran while one was open for 0% of the time, Pallas kernels for 0%

profile of v1, /device:TPU:448, one launch (start us, length us, event | category | flops | bytes accessed | tf_op | source)
XLA Modules:
  0.0 159.8 jit_solution(10344534938554481083)
XLA Ops:
  0.0 0.0 copy-start
  0.0 0.0 copy-start.10
  0.0 1.4 fusion.2
  1.4 1.9 %collective-permute-start = (bf16[32,64,128]{2,1,0:T(8,128)(2,1)S(1)}, bf16[32,64,128]{2,1,0:T(8,128)(2,1)S(1)}, u32[]{:S(2)}, u32[]{:S(2)}) collective-permute-start(bf16[32,64,128]{2,1,0:T(8,128)(2,1)S(1)} %get-tuple-element.10), channel_id=1, source_target_pairs={{0,8},{8,16},{16,24},{24,32},{32,40},{40,48},{48,56},{56,64},{64,7... | collective-permute-start | bytes 1572872 | tf_op jit(solution)/shard_map/ppermute | solution.py:212
  3.3 6.7 %collective-permute-start.1 = (bf16[32,64,128]{2,1,0:T(8,128)(2,1)S(1)}, bf16[32,64,128]{2,1,0:T(8,128)(2,1)S(1)}, u32[]{:S(2)}, u32[]{:S(2)}) collective-permute-start(bf16[32,64,128]{2,1,0:T(8,128)(2,1)S(1)} %get-tuple-element.9), channel_id=1, source_target_pairs={{8,0},{16,8},{24,16},{32,24},{40,32},{48,40},{56,48},{64,56},{72,6... | collective-permute-start | bytes 1572872 | tf_op jit(solution)/shard_map/ppermute | solution.py:213
  10.0 0.0 copy-done.10
  10.0 0.0 copy-start.12
  10.0 0.0 copy-start.11
  10.0 0.1 copy.15
  10.1 0.6 copy-done.12
  10.7 0.1 dynamic_slice.9
  10.8 0.0 copy-done.11
  10.8 0.1 compare_and_fusion
  10.9 0.1 pad_dynamic-slice_fusion.1
  11.0 0.0 copy-start.3
  11.0 0.0 copy-start.4
  11.0 0.2 select_convert_fusion.bias
  11.2 6.4 %collective-permute-done.before = bf16[32,64,128]{2,1,0:T(8,128)(2,1)S(1)} collective-permute-done((bf16[32,64,128]{2,1,0:T(8,128)(2,1)S(1)}, bf16[32,64,128]{2,1,0:T(8,128)(2,1)S(1)}, u32[]{:S(2)}, u32[]{:S(2)}) %collective-permute-start) | collective-permute-done | bytes 524320 | tf_op jit(solution)/shard_map/ppermute | solution.py:212
  17.6 4.6 %collective-permute-done.1.after = bf16[32,64,128]{2,1,0:T(8,128)(2,1)S(1)} collective-permute-done((bf16[32,64,128]{2,1,0:T(8,128)(2,1)S(1)}, bf16[32,64,128]{2,1,0:T(8,128)(2,1)S(1)}, u32[]{:S(2)}, u32[]{:S(2)}) %collective-permute-start.1) | collective-permute-done | bytes 524320 | tf_op jit(solution)/shard_map/ppermute | solution.py:213
  22.3 0.0 copy-start.8
  22.3 0.0 copy-start.9
  22.3 0.0 copy-done
  22.3 0.0 copy-done.3
  22.3 0.0 copy-done.4
  22.3 0.6 copy-done.8
  22.9 0.0 copy-done.9
  22.9 52.5 %time_stage.1 = (bf16[32,128,128]{2,1,0:T(8,128)(2,1)S(1)}, bf16[128,32,128]{2,1,0:T(8,128)(2,1)}) custom-call(bf16[32,64,128]{2,1,0:T(8,128)(2,1)S(1)} %collective-permute-done.before, bf16[32,128,128]{2,1,0:T(8,128)(2,1)S(1)} %copy-done, bf16[32,64,128]{2,1,0:T(8,128)(2,1)S(1)} %collective-permute-done.1.after, ...), custom_call_target="tpu_custom_call" | custom-call | tf_op jit(solution)/shard_map/time_stage/pallas_call | solution.py:125
  75.5 0.0 copy-start.13
  75.5 4.4 %all-to-all-start = ((bf16[128,32,128]{2,1,0:T(8,128)(2,1)}), bf16[128,32,128]{2,1,0:T(8,128)(2,1)S(1)}, u32[]{:S(2)}, u32[]{:S(2)}) async-start(bf16[128,32,128]{2,1,0:T(8,128)(2,1)} %get-tuple-element.7), calls=%async_computation | async-start | bytes 2097152 | tf_op jit(solution)/shard_map/all_to_all | solution.py:227
  79.9 0.0 copy-done.13
  79.9 0.0 copy-start.5
  79.9 0.1 copy.16
  80.0 15.6 %all-to-all-done = bf16[128,32,128]{2,1,0:T(8,128)(2,1)S(1)} async-done(((bf16[128,32,128]{2,1,0:T(8,128)(2,1)}), bf16[128,32,128]{2,1,0:T(8,128)(2,1)S(1)}, u32[]{:S(2)}, u32[]{:S(2)}) %all-to-all-start) | async-done | bytes 1048608 | tf_op jit(solution)/shard_map/all_to_all | solution.py:227
  95.7 0.0 copy-done.5
  95.7 24.3 %freq_stage.1 = bf16[8,16,32,128]{3,2,1,0:T(8,128)(2,1)S(1)} custom-call(bf16[8,16,32,128]{3,2,1,0:T(8,128)(2,1)S(1)} %bitcast.7, bf16[128,128]{1,0:T(8,128)(2,1)S(1)} %copy-done.5, bf16[128,128]{1,0:T(8,128)(2,1)S(1)} %bitcast.10), custom_call_target="tpu_custom_call" | custom-call | tf_op jit(solution)/shard_map/freq_stage/pallas_call | solution.py:144
  120.0 0.0 copy-start.1
  120.0 0.0 copy-start.2
  120.0 0.0 copy-start.6
  120.0 19.5 %all_to_all.10.mixed = bf16[128,32,128]{2,1,0:T(8,128)(2,1)S(1)} all-to-all(bf16[128,32,128]{2,1,0:T(8,128)(2,1)S(1)} %bitcast.8), channel_id=1, replica_groups=mesh['tm'=64,'freq'=8] {'freq'}, dimensions={0} | all-to-all | bytes 2097152 | tf_op jit(solution)/shard_map/all_to_all | solution.py:231
  139.5 0.0 copy-start.7
  139.5 0.0 copy-done.1
  139.6 0.0 copy-done.2
  139.6 0.0 copy-done.6
  139.6 0.6 copy-done.7
  140.2 19.6 %mlp_stage.1 = bf16[32,128,128]{2,1,0:T(8,128)(2,1)} custom-call(bf16[128,32,128]{2,1,0:T(8,128)(2,1)S(1)} %all_to_all.10.mixed, bf16[32,128,128]{2,1,0:T(8,128)(2,1)S(1)} %get-tuple-element.8.after_time, bf16[128,128]{1,0:T(8,128)(2,1)S(1)} %copy-done.6, f32[1,128]{1,0:T(1,128)S(1)} %bitcast.11, bf16[128,512]{1,0:T(8,128)(2,1)S(1)} %copy-done.1, ...), custom_call_target="tpu_custom_call" | custom-call | tf_op jit(solution)/shard_map/mlp_stage/pallas_call | solution.py:157
  (2 shorter events, 0.0 us)
Async XLA Ops:
  0.0 22.3 %copy-start = (bf16[32,128,128]{2,1,0:T(8,128)(2,1)S(1)}, bf16[32,128,128]{2,1,0:T(8,128)(2,1)}, u32[]{:S(2)}) copy-start(bf16[32,128,128]{2,1,0:T(8,128)(2,1)} %own.1) | copy-start | bytes 3145732
  0.0 10.0 %copy-start.10 = (bf16[128,128]{1,0:T(8,128)(2,1)S(1)}, bf16[128,128]{1,0:T(8,128)(2,1)}, u32[]{:S(2)}) copy-start(bf16[128,128]{1,0:T(8,128)(2,1)} %param.19) | copy-start | bytes 98308
  1.4 16.3 %collective-permute-start = (bf16[32,64,128]{2,1,0:T(8,128)(2,1)S(1)}, bf16[32,64,128]{2,1,0:T(8,128)(2,1)S(1)}, u32[]{:S(2)}, u32[]{:S(2)}) collective-permute-start(bf16[32,64,128]{2,1,0:T(8,128)(2,1)S(1)} %get-tuple-element.10), channel_id=1, source_target_pairs={{0,8},{8,16},{16,24},{24,32},{32,40},{40,48},{48,56},{56,64},{64,7... | collective-permute-start | bytes 1572872 | tf_op jit(solution)/shard_map/ppermute | solution.py:212
  3.3 19.0 %collective-permute-start.1 = (bf16[32,64,128]{2,1,0:T(8,128)(2,1)S(1)}, bf16[32,64,128]{2,1,0:T(8,128)(2,1)S(1)}, u32[]{:S(2)}, u32[]{:S(2)}) collective-permute-start(bf16[32,64,128]{2,1,0:T(8,128)(2,1)S(1)} %get-tuple-element.9), channel_id=1, source_target_pairs={{8,0},{16,8},{24,16},{32,24},{40,32},{48,40},{56,48},{64,56},{72,6... | collective-permute-start | bytes 1572872 | tf_op jit(solution)/shard_map/ppermute | solution.py:213
  10.0 0.8 copy-start.12
  10.0 0.8 copy-start.11
  11.0 11.3 %copy-start.3 = (bf16[128,128]{1,0:T(8,128)(2,1)S(1)}, bf16[128,128]{1,0:T(8,128)(2,1)}, u32[]{:S(2)}) copy-start(bf16[128,128]{1,0:T(8,128)(2,1)} %match.2) | copy-start | bytes 98308
  11.0 11.3 %copy-start.4 = (bf16[128,128]{1,0:T(8,128)(2,1)S(1)}, bf16[128,128]{1,0:T(8,128)(2,1)}, u32[]{:S(2)}) copy-start(bf16[128,128]{1,0:T(8,128)(2,1)} %out_w.2) | copy-start | bytes 98308
  22.3 0.7 copy-start.8
  22.3 0.7 copy-start.9
  75.5 4.4 %copy-start.13 = (bf16[128,128]{1,0:T(8,128)(2,1)S(1)}, bf16[128,128]{1,0:T(8,128)(2,1)}, u32[]{:S(2)}) copy-start(bf16[128,128]{1,0:T(8,128)(2,1)} %param.23) | copy-start | bytes 98308
  75.5 20.2 %all-to-all-start = ((bf16[128,32,128]{2,1,0:T(8,128)(2,1)}), bf16[128,32,128]{2,1,0:T(8,128)(2,1)S(1)}, u32[]{:S(2)}, u32[]{:S(2)}) async-start(bf16[128,32,128]{2,1,0:T(8,128)(2,1)} %get-tuple-element.7), calls=%async_computation | async-start | bytes 2097152 | tf_op jit(solution)/shard_map/all_to_all | solution.py:227
  79.9 15.8 %copy-start.5 = (bf16[128,128]{1,0:T(8,128)(2,1)S(1)}, bf16[128,128]{1,0:T(8,128)(2,1)}, u32[]{:S(2)}) copy-start(bf16[128,128]{1,0:T(8,128)(2,1)} %match.3) | copy-start | bytes 98308
  120.0 19.6 %copy-start.1 = (bf16[128,512]{1,0:T(8,128)(2,1)S(1)}, bf16[128,512]{1,0:T(8,128)(2,1)}, u32[]{:S(2)}) copy-start(bf16[128,512]{1,0:T(8,128)(2,1)} %up.1) | copy-start | bytes 393220
  120.0 19.6 %copy-start.2 = (bf16[512,128]{1,0:T(8,128)(2,1)S(1)}, bf16[512,128]{1,0:T(8,128)(2,1)}, u32[]{:S(2)}) copy-start(bf16[512,128]{1,0:T(8,128)(2,1)} %down.1) | copy-start | bytes 393220
  120.0 19.6 %copy-start.6 = (bf16[128,128]{1,0:T(8,128)(2,1)S(1)}, bf16[128,128]{1,0:T(8,128)(2,1)}, u32[]{:S(2)}) copy-start(bf16[128,128]{1,0:T(8,128)(2,1)} %out_w.3) | copy-start | bytes 98308
  139.5 0.7 copy-start.7

commit v2 on v1

v2 whole, which is shorter than its diff:
```python
import functools
import math

import jax
import jax.numpy as jnp
from jax import lax
from jax.experimental import pallas as pl
from jax.experimental.pallas import tpu as pltpu
from jax.sharding import PartitionSpec as P

HEADS = 4
HALO = 64
PROJECT_BINS = 4
FINISH_BINS = 4
MLP_BINS = 4
TURN_STEPS = 4
F32 = jnp.float32
BF16 = jnp.bfloat16
NEG = -1e30
ONES_ROWS = 16


def layer_norm(values, gain):
    widened = values.astype(F32)
    centred = widened - jnp.mean(widened, -1, keepdims=True)
    spread = jnp.mean(centred * centred, -1, keepdims=True)
    return (centred * lax.rsqrt(spread + 1e-05) * gain).astype(BF16)


def dot_nt(a, b):
    return lax.dot_general(a, b, (((1,), (1,)), ((), ())), preferred_element_type=F32)


def dot_tn(a, b):
    return lax.dot_general(a, b, (((0,), (0,)), ((), ())), preferred_element_type=F32)


def dot_nn(a, b):
    return jnp.dot(a, b, preferred_element_type=F32)


def head_scales(width):
    head = lax.broadcasted_iota(jnp.int32, (1, width), 1) // (width // HEADS)
    scale = (width // HEADS) ** (-0.5) * math.log2(math.e)
    return [jnp.where(head == h, scale, 0.0).astype(F32) for h in range(HEADS)]


def extended(values_t):
    return jnp.concatenate([values_t, jnp.ones((ONES_ROWS, values_t.shape[1]), BF16)], 0)


def score(key_rows, sides, bias, scores, largest):
    found = dot_nt(key_rows, jnp.concatenate(sides, 0))
    if bias is not None:
        found = found + bias
    scores[...] = found
    largest[...] = jnp.max(found, 0, keepdims=True)


def weigh(scores, largest, weights):
    weights[...] = jnp.exp2(scores[...] - largest[...]).astype(BF16)


def gather(values_t, weights, heads, columns):
    depth = values_t.shape[0] // heads
    pieces = []
    for h in range(heads):
        mixed = dot_nn(extended(values_t[h * depth : (h + 1) * depth]), weights[:, h * columns : (h + 1) * columns])
        pieces.append(mixed[:depth] / mixed[depth : depth + 1])
    return jnp.concatenate(pieces, 0).astype(BF16)


def time_kernel(
    before, own, after, bias, time_gain, match, value_t, out_w, freq_gain,
    after_time, sent, keys, values, mixes, turned, s0, s1, m0, m1, e0, e1,
):
    bins, count, width = own.shape
    span = count + 2 * HALO
    scales = head_scales(width)

    def project(i, carry):
        parts = []
        for j in range(PROJECT_BINS):
            b = i * PROJECT_BINS + j
            parts += [before[b], own[b], after[b]]
        normed = layer_norm(jnp.concatenate(parts, 0), time_gain[...])
        keys[pl.ds(i * PROJECT_BINS, PROJECT_BINS)] = (
            dot_nn(normed, match[...]).astype(BF16).reshape(PROJECT_BINS, span, width)
        )
        found = dot_nt(value_t[...], normed).astype(BF16)
        for j in range(PROJECT_BINS):
            values[i * PROJECT_BINS + j] = found[:, j * span : (j + 1) * span]
        return carry

    lax.fori_loop(0, bins // PROJECT_BINS, project, 0)

    def score_bin(b, scores, largest):
        rows = keys[b]
        wide = rows[HALO : HALO + count].astype(F32)
        sides = [(wide * scale).astype(BF16) for scale in scales]
        score(rows, sides, jnp.concatenate([bias[...]] * HEADS, 1), scores, largest)

    def gather_bin(b, weights):
        mixes[b + 2] = gather(values[jnp.maximum(b, 0)], weights, HEADS, count)

    def attend(i, carry):
        b = jnp.minimum(2 * i, bins - 2)
        score_bin(b, s0, m0)
        weigh(s1, m1, e1)
        gather_bin(2 * i - 2, e0)
        score_bin(b + 1, s1, m1)
        weigh(s0, m0, e0)
        gather_bin(2 * i - 1, e1)
        return carry

    lax.fori_loop(0, bins // 2 + 1, attend, 0)

    def finish(i, carry):
        parts = [dot_tn(mixes[i * FINISH_BINS + j + 2], out_w[...]) for j in range(FINISH_BINS)]
        first = i * FINISH_BINS
        spec = own[pl.ds(first, FINISH_BINS)].astype(F32).reshape(FINISH_BINS * count, width)
        result = (spec + jnp.concatenate(parts, 0)).astype(BF16)
        after_time[pl.ds(first, FINISH_BINS)] = result.reshape(FINISH_BINS, count, width)
        normed = layer_norm(result, freq_gain[...]).astype(F32)
        for j in range(FINISH_BINS):
            turned[pl.ds(first + j, count, stride=bins), :] = normed[j * count : (j + 1) * count]
        return carry

    lax.fori_loop(0, bins // FINISH_BINS, finish, 0)

    def turn(i, carry):
        rows = count // TURN_STEPS
        found = turned[pl.ds(i * rows * bins, rows * bins), :]
        sent[pl.ds(i * rows, rows)] = found.astype(BF16).reshape(rows, bins, width)
        return carry

    lax.fori_loop(0, TURN_STEPS, turn, 0)


def freq_kernel(rows, match, value_t, mixed_out, keys, values, mixes, s0, s1, m0, m1, e0, e1):
    parts, frames, each, width = rows.shape
    bins = parts * each
    scales = head_scales(width)
    half = HEADS // 2

    def project(i, carry):
        normed = jnp.concatenate(
            [rows[:, i * PROJECT_BINS + j].reshape(bins, width) for j in range(PROJECT_BINS)], 0
        )
        keys[pl.ds(i * PROJECT_BINS, PROJECT_BINS)] = (
            dot_nn(normed, match[...]).astype(BF16).reshape(PROJECT_BINS, bins, width)
        )
        found = dot_nt(value_t[...], normed).astype(BF16)
        for j in range(PROJECT_BINS):
            values[i * PROJECT_BINS + j] = found[:, j * bins : (j + 1) * bins]
        return carry

    lax.fori_loop(0, frames // PROJECT_BINS, project, 0)

    def score_pair(f, pair, scores, largest):
        wide = keys[f].astype(F32)
        sides = [(wide * scale).astype(BF16) for scale in scales[pair * half : (pair + 1) * half]]
        score(keys[f], sides, None, scores, largest)

    def gather_pair(f, pair, weights):
        low, high = pair * width // 2, (pair + 1) * width // 2
        mixes[f + 1, low:high] = gather(values[jnp.maximum(f, 0), low:high], weights, half, bins)

    def attend(i, carry):
        f = jnp.minimum(i, frames - 1)
        score_pair(f, 0, s0, m0)
        weigh(s1, m1, e1)
        gather_pair(i - 1, 0, e0)
        score_pair(f, 1, s1, m1)
        weigh(s0, m0, e0)
        gather_pair(i - 1, 1, e1)
        return carry

    lax.fori_loop(0, frames + 1, attend, 0)

    def finish(f, carry):
        mixed_out[:, f] = mixes[f + 1].T.reshape(parts, each, width)
        return carry

    lax.fori_loop(0, frames, finish, 0, unroll=2)


def mlp_kernel(mixed, after_time, out_w, gain, up, down, block_out, turned):
    count, bins, width = mixed.shape

    def turn(i, carry):
        rows = count // TURN_STEPS
        found = mixed[pl.ds(i * rows, rows)].astype(F32).reshape(rows * bins, width)
        turned[pl.ds(i * rows * bins, rows * bins), :] = found
        return carry

    lax.fori_loop(0, TURN_STEPS, turn, 0)

    def some_bins(i, carry):
        first = i * MLP_BINS
        mix = jnp.concatenate(
            [turned[pl.ds(first + j, count, stride=bins), :] for j in range(MLP_BINS)], 0
        ).astype(BF16)
        base = after_time[pl.ds(first, MLP_BINS)].astype(F32).reshape(MLP_BINS * count, width)
        after_freq = (base + dot_nn(mix, out_w[...])).astype(BF16)
        hidden = jax.nn.gelu(dot_nn(layer_norm(after_freq, gain[...]), up[...])).astype(BF16)
        result = (after_freq.astype(F32) + dot_nn(hidden, down[...])).astype(BF16)
        block_out[pl.ds(first, MLP_BINS)] = result.reshape(MLP_BINS, count, width)
        return carry

    lax.fori_loop(0, bins // MLP_BINS, some_bins, 0)


def full(array):
    return pl.BlockSpec(array.shape, lambda i: (0,) * array.ndim)


def params():
    return pltpu.CompilerParams(dimension_semantics=("arbitrary",), vmem_limit_bytes=48 << 20)


def buffers(keys, columns):
    return (
        [pltpu.VMEM((keys, columns), F32)] * 2
        + [pltpu.VMEM((1, columns), F32)] * 2
        + [pltpu.VMEM((keys, columns), BF16)] * 2
    )


def time_stage(before, spec, after, bias, time_gain, match, value_t, out_w, freq_gain):
    bins, count, width = spec.shape
    span = count + 2 * HALO
    args = (before, spec, after, bias, time_gain, match, value_t, out_w, freq_gain)
    shapes = [(bins, count, width), (count, bins, width)]
    return pl.pallas_call(
        time_kernel,
        grid=(1,),
        in_specs=[full(a) for a in args],
        out_specs=[pl.BlockSpec(s, lambda i: (0, 0, 0)) for s in shapes],
        out_shape=[jax.ShapeDtypeStruct(s, BF16) for s in shapes],
        scratch_shapes=[
            pltpu.VMEM((bins, span, width), BF16),
            pltpu.VMEM((bins, width, span), BF16),
            pltpu.VMEM((bins + 2, width, count), BF16),
            pltpu.VMEM((count * bins, width), F32),
        ]
        + buffers(span, HEADS * count),
        compiler_params=params(),
        name="time_stage",
    )(*args)


def freq_stage(rows, match, value_t):
    parts, frames, each, width = rows.shape
    bins = parts * each
    return pl.pallas_call(
        freq_kernel,
        grid=(1,),
        in_specs=[full(rows), full(match), full(value_t)],
        out_specs=full(rows),
        out_shape=jax.ShapeDtypeStruct(rows.shape, BF16),
        scratch_shapes=[
            pltpu.VMEM((frames, bins, width), BF16),
            pltpu.VMEM((frames, width, bins), BF16),
            pltpu.VMEM((frames + 1, width, bins), BF16),
        ]
        + buffers(bins, HEADS // 2 * bins),
        compiler_params=params(),
        name="freq_stage",
    )(rows, match, value_t)


def mlp_stage(mixed, after_time, out_w, gain, up, down):
    bins, count, width = after_time.shape
    args = (mixed, after_time, out_w, gain, up, down)
    return pl.pallas_call(
        mlp_kernel,
        grid=(1,),
        in_specs=[full(a) for a in args],
        out_specs=full(after_time),
        out_shape=jax.ShapeDtypeStruct((bins, count, width), BF16),
        scratch_shapes=[pltpu.VMEM((count * bins, width), F32)],
        compiler_params=params(),
        name="mlp_stage",
    )(*args)


def key_bias(segment_ids, active, count):
    frames = segment_ids.shape[0]
    span = count + 2 * HALO
    start = lax.axis_index("tm") * count
    seg_query = lax.dynamic_slice_in_dim(segment_ids, start, count, 0)
    seg_key = lax.dynamic_slice_in_dim(jnp.pad(segment_ids, HALO, constant_values=-1), start, span, 0)
    act_key = lax.dynamic_slice_in_dim(jnp.pad(active, HALO), start, span, 0)
    pos_key = start - HALO + jnp.arange(span, dtype=jnp.int32)
    pos_query = start + jnp.arange(count, dtype=jnp.int32)
    inside = (pos_key >= 0) & (pos_key < frames)
    allowed = (
        inside[:, None]
        & (seg_query[None, :] == seg_key[:, None])
        & ((act_key[:, None] == 1) | (pos_query[None, :] == pos_key[:, None]))
    )
    return jnp.where(allowed, 0.0, NEG).astype(F32)


def per_device(
    spec,
    segment_ids,
    active,
    time_gain,
    time_match,
    time_value,
    time_out,
    freq_gain,
    freq_match,
    freq_value,
    freq_out,
    mlp_gain,
    mlp_up,
    mlp_down,
):
    bins, count, width = spec.shape
    peers = lax.axis_size("tm")
    split = lax.axis_size("freq")
    up = [(i, i + 1) for i in range(peers - 1)]
    down = [(j, i) for i, j in up]
    before = lax.ppermute(spec[:, count - HALO :], "tm", up)
    after = lax.ppermute(spec[:, :HALO], "tm", down)
    bias = key_bias(segment_ids, active, count)
    after_time, sent = time_stage(
        before,
        spec,
        after,
        bias,
        time_gain[None],
        time_match,
        time_value.T,
        time_out,
        freq_gain[None],
    )
    gathered = lax.all_to_all(sent, "freq", split_axis=0, concat_axis=0, tiled=True)
    mixed = freq_stage(
        gathered.reshape(split, count // split, bins, width), freq_match, freq_value.T
    )
    returned = lax.all_to_all(
        mixed.reshape(count, bins, width), "freq", split_axis=0, concat_axis=0, tiled=True
    )
    return mlp_stage(returned, after_time, freq_out, mlp_gain[None], mlp_up, mlp_down)


def solution(mesh):
    placed = (P("freq", "tm", None),) + (P(),) * 13
    return jax.shard_map(
        per_device, mesh=mesh, in_specs=placed, out_specs=P("freq", "tm", None), check_vma=False
    )
```

time: 160 us -> 102 us (0.64)
  Pallas kernels: 96.4 us -> 38.2 us
    pallas_call x3, Pallas kernels: 96.4 us -> 38.2 us  [the longest x1 20.2 us: time_stage(): pl.pallas_call(time_kernel, grid=(1,), in_specs=[full(a) for a in args],...]
  transfers between devices with their start and end apart: 3 -> 3, of which waited for: 3 -> 3; matrix products, arithmetic and copies ran while one was open for 0% -> 1% of each run, Pallas kernels for 0% -> 0%
where the time goes in v2:
time: 102 us
  Pallas kernels  38.2 us (37%)
  waiting for transfers between devices  26.7 us (26%)
  blocking collectives  19.5 us (19%)
  starting transfers between devices  13 us (13%)
  local copies, waits for them, and re-layouts  3.64 us (4%)
    pallas_call x1, Pallas kernels, time_stage(): pl.pallas_call(time_kernel, grid=(1,), in_specs=[full(a) for a in args],...  20.2 us
    all_to_all x1, blocking collectives, per_device(): lax.all_to_all(mixed.reshape(count, bins, width), 'freq', split_axis=0, c...  19.5 us
    all_to_all x1, waiting for transfers between devices, per_device(): lax.all_to_all(sent, 'freq', split_axis=0, concat_axis=0, tiled=True)  15.6 us
    pallas_call x1, Pallas kernels, mlp_stage(): pl.pallas_call(mlp_kernel, grid=(1,), in_specs=[full(a) for a in args], o...  9.29 us
    pallas_call x1, Pallas kernels, freq_stage(): pl.pallas_call(freq_kernel, grid=(1,), in_specs=[full(rows), full(match),...  8.69 us
    ppermute x1, starting transfers between devices, per_device(): after = lax.ppermute(spec[:, :HALO], 'tm', down)  6.65 us
    ppermute x1, waiting for transfers between devices, per_device(): before = lax.ppermute(spec[:, count - HALO:], 'tm', up)  6.43 us
    ppermute x1, waiting for transfers between devices, per_device(): after = lax.ppermute(spec[:, :HALO], 'tm', down)  4.63 us
  transfers between devices with their start and end apart: 3, of which 3 were waited for; matrix products, arithmetic and copies ran while one was open for 1% of the time, Pallas kernels for 0%

profile of v2, /device:TPU:448, one launch (start us, length us, event | category | flops | bytes accessed | tf_op | source)
XLA Modules:
  0.0 101.5 jit_solution(11708113685768959501)
XLA Ops:
  0.0 0.0 copy-start
  0.0 0.0 copy-start.10
  0.0 1.4 %fusion.1 = (bf16[32,64,128]{2,1,0:T(8,128)(2,1)S(1)}, bf16[32,64,128]{2,1,0:T(8,128)(2,1)S(1)}) fusion(bf16[32,128,128]{2,1,0:T(8,128)(2,1)} %own.1), kind=kLoop, calls=%fused_computation.7 | loop fusion | bytes 2097152 | tf_op jit(solution)/shard_map/slice | solution.py:328
  1.4 1.9 %collective-permute-start = (bf16[32,64,128]{2,1,0:T(8,128)(2,1)S(1)}, bf16[32,64,128]{2,1,0:T(8,128)(2,1)S(1)}, u32[]{:S(2)}, u32[]{:S(2)}) collective-permute-start(bf16[32,64,128]{2,1,0:T(8,128)(2,1)S(1)} %get-tuple-element.10), channel_id=1, source_target_pairs={{0,8},{8,16},{16,24},{24,32},{32,40},{40,48},{48,56},{56,64},{64,7... | collective-permute-start | bytes 1572872 | tf_op jit(solution)/shard_map/ppermute | solution.py:327
  3.3 6.7 %collective-permute-start.1 = (bf16[32,64,128]{2,1,0:T(8,128)(2,1)S(1)}, bf16[32,64,128]{2,1,0:T(8,128)(2,1)S(1)}, u32[]{:S(2)}, u32[]{:S(2)}) collective-permute-start(bf16[32,64,128]{2,1,0:T(8,128)(2,1)S(1)} %get-tuple-element.9), channel_id=1, source_target_pairs={{8,0},{16,8},{24,16},{32,24},{40,32},{48,40},{56,48},{64,56},{72,6... | collective-permute-start | bytes 1572872 | tf_op jit(solution)/shard_map/ppermute | solution.py:328
  10.0 0.0 copy-done.10
  10.0 0.0 copy-start.12
  10.0 0.0 copy-start.11
  10.0 0.1 copy.15
  10.1 0.6 copy-done.12
  10.7 0.1 dynamic_slice.9
  10.8 0.0 copy-done.11
  10.8 0.1 compare_and_fusion
  10.9 0.1 pad_dynamic-slice_fusion.1
  11.0 0.0 copy-start.3
  11.0 0.0 copy-start.4
  11.0 0.2 and_select_fusion.bias
  11.2 6.4 %collective-permute-done.before = bf16[32,64,128]{2,1,0:T(8,128)(2,1)S(1)} collective-permute-done((bf16[32,64,128]{2,1,0:T(8,128)(2,1)S(1)}, bf16[32,64,128]{2,1,0:T(8,128)(2,1)S(1)}, u32[]{:S(2)}, u32[]{:S(2)}) %collective-permute-start) | collective-permute-done | bytes 524320 | tf_op jit(solution)/shard_map/ppermute | solution.py:327
  17.6 4.6 %collective-permute-done.1.after = bf16[32,64,128]{2,1,0:T(8,128)(2,1)S(1)} collective-permute-done((bf16[32,64,128]{2,1,0:T(8,128)(2,1)S(1)}, bf16[32,64,128]{2,1,0:T(8,128)(2,1)S(1)}, u32[]{:S(2)}, u32[]{:S(2)}) %collective-permute-start.1) | collective-permute-done | bytes 524320 | tf_op jit(solution)/shard_map/ppermute | solution.py:328
  22.3 0.0 copy-start.8
  22.3 0.0 copy-start.9
  22.3 0.0 copy-done
  22.3 0.0 copy-done.3
  22.3 0.0 copy-done.4
  22.3 0.6 copy-done.8
  22.9 0.0 copy-done.9
  22.9 20.2 %time_stage.1 = (bf16[32,128,128]{2,1,0:T(8,128)(2,1)S(1)}, bf16[128,32,128]{2,1,0:T(8,128)(2,1)}) custom-call(bf16[32,64,128]{2,1,0:T(8,128)(2,1)S(1)} %collective-permute-done.before, bf16[32,128,128]{2,1,0:T(8,128)(2,1)S(1)} %copy-done, bf16[32,64,128]{2,1,0:T(8,128)(2,1)S(1)} %collective-permute-done.1.after, f32[256,128]{1,0:T(8,128)S(1)} %and_select_fusion.bias, ...), custom_call_target="tpu_custom_call" | custom-call | tf_op jit(solution)/shard_map/time_stage/pallas_call | solution.py:235
  43.2 0.0 copy-start.13
  43.2 4.4 %all-to-all-start = ((bf16[128,32,128]{2,1,0:T(8,128)(2,1)}), bf16[128,32,128]{2,1,0:T(8,128)(2,1)S(1)}, u32[]{:S(2)}, u32[]{:S(2)}) async-start(bf16[128,32,128]{2,1,0:T(8,128)(2,1)} %get-tuple-element.7), calls=%async_computation | async-start | bytes 2097152 | tf_op jit(solution)/shard_map/all_to_all | solution.py:341
  47.6 0.0 copy-done.13
  47.6 0.0 copy-start.5
  47.6 0.1 copy.16
  47.7 15.6 %all-to-all-done = bf16[128,32,128]{2,1,0:T(8,128)(2,1)S(1)} async-done(((bf16[128,32,128]{2,1,0:T(8,128)(2,1)}), bf16[128,32,128]{2,1,0:T(8,128)(2,1)S(1)}, u32[]{:S(2)}, u32[]{:S(2)}) %all-to-all-start) | async-done | bytes 1048608 | tf_op jit(solution)/shard_map/all_to_all | solution.py:341
  63.4 0.0 copy-done.5
  63.4 8.7 %freq_stage.1 = bf16[8,16,32,128]{3,2,1,0:T(8,128)(2,1)S(1)} custom-call(bf16[8,16,32,128]{3,2,1,0:T(8,128)(2,1)S(1)} %bitcast.7, bf16[128,128]{1,0:T(8,128)(2,1)S(1)} %copy-done.5, bf16[128,128]{1,0:T(8,128)(2,1)S(1)} %bitcast.10), custom_call_target="tpu_custom_call" | custom-call | tf_op jit(solution)/shard_map/freq_stage/pallas_call | solution.py:256
  72.1 0.0 copy-start.1
  72.1 0.0 copy-start.2
  72.1 0.0 copy-start.6
  72.1 19.5 %all_to_all.10.mixed = bf16[128,32,128]{2,1,0:T(8,128)(2,1)S(1)} all-to-all(bf16[128,32,128]{2,1,0:T(8,128)(2,1)S(1)} %bitcast.8), channel_id=1, replica_groups=mesh['tm'=64,'freq'=8] {'freq'}, dimensions={0} | all-to-all | bytes 2097152 | tf_op jit(solution)/shard_map/all_to_all | solution.py:345
  91.6 0.0 copy-start.7
  91.6 0.0 copy-done.1
  91.6 0.0 copy-done.2
  91.6 0.0 copy-done.6
  91.6 0.6 copy-done.7
  92.3 9.3 %mlp_stage.1 = bf16[32,128,128]{2,1,0:T(8,128)(2,1)} custom-call(bf16[128,32,128]{2,1,0:T(8,128)(2,1)S(1)} %all_to_all.10.mixed, bf16[32,128,128]{2,1,0:T(8,128)(2,1)S(1)} %get-tuple-element.8.after_time, bf16[128,128]{1,0:T(8,128)(2,1)S(1)} %copy-done.6, f32[1,128]{1,0:T(1,128)S(1)} %bitcast.11, bf16[128,512]{1,0:T(8,128)(2,1)S(1)} %copy-done.1, ...), custom_call_target="tpu_custom_call" | custom-call | tf_op jit(solution)/shard_map/mlp_stage/pallas_call | solution.py:276
  (1 shorter events, 0.0 us)
Async XLA Ops:
  0.0 22.3 %copy-start = (bf16[32,128,128]{2,1,0:T(8,128)(2,1)S(1)}, bf16[32,128,128]{2,1,0:T(8,128)(2,1)}, u32[]{:S(2)}) copy-start(bf16[32,128,128]{2,1,0:T(8,128)(2,1)} %own.1) | copy-start | bytes 3145732
  0.0 10.0 %copy-start.10 = (bf16[128,128]{1,0:T(8,128)(2,1)S(1)}, bf16[128,128]{1,0:T(8,128)(2,1)}, u32[]{:S(2)}) copy-start(bf16[128,128]{1,0:T(8,128)(2,1)} %param.19) | copy-start | bytes 98308
  1.4 16.3 %collective-permute-start = (bf16[32,64,128]{2,1,0:T(8,128)(2,1)S(1)}, bf16[32,64,128]{2,1,0:T(8,128)(2,1)S(1)}, u32[]{:S(2)}, u32[]{:S(2)}) collective-permute-start(bf16[32,64,128]{2,1,0:T(8,128)(2,1)S(1)} %get-tuple-element.10), channel_id=1, source_target_pairs={{0,8},{8,16},{16,24},{24,32},{32,40},{40,48},{48,56},{56,64},{64,7... | collective-permute-start | bytes 1572872 | tf_op jit(solution)/shard_map/ppermute | solution.py:327
  3.3 19.0 %collective-permute-start.1 = (bf16[32,64,128]{2,1,0:T(8,128)(2,1)S(1)}, bf16[32,64,128]{2,1,0:T(8,128)(2,1)S(1)}, u32[]{:S(2)}, u32[]{:S(2)}) collective-permute-start(bf16[32,64,128]{2,1,0:T(8,128)(2,1)S(1)} %get-tuple-element.9), channel_id=1, source_target_pairs={{8,0},{16,8},{24,16},{32,24},{40,32},{48,40},{56,48},{64,56},{72,6... | collective-permute-start | bytes 1572872 | tf_op jit(solution)/shard_map/ppermute | solution.py:328
  10.0 0.8 copy-start.12
  10.0 0.8 copy-start.11
  11.0 11.3 %copy-start.3 = (bf16[128,128]{1,0:T(8,128)(2,1)S(1)}, bf16[128,128]{1,0:T(8,128)(2,1)}, u32[]{:S(2)}) copy-start(bf16[128,128]{1,0:T(8,128)(2,1)} %match.2) | copy-start | bytes 98308
  11.0 11.3 %copy-start.4 = (bf16[128,128]{1,0:T(8,128)(2,1)S(1)}, bf16[128,128]{1,0:T(8,128)(2,1)}, u32[]{:S(2)}) copy-start(bf16[128,128]{1,0:T(8,128)(2,1)} %out_w.2) | copy-start | bytes 98308
  22.3 0.7 copy-start.8
  22.3 0.7 copy-start.9
  43.2 4.4 %copy-start.13 = (bf16[128,128]{1,0:T(8,128)(2,1)S(1)}, bf16[128,128]{1,0:T(8,128)(2,1)}, u32[]{:S(2)}) copy-start(bf16[128,128]{1,0:T(8,128)(2,1)} %param.23) | copy-start | bytes 98308
  43.2 20.2 %all-to-all-start = ((bf16[128,32,128]{2,1,0:T(8,128)(2,1)}), bf16[128,32,128]{2,1,0:T(8,128)(2,1)S(1)}, u32[]{:S(2)}, u32[]{:S(2)}) async-start(bf16[128,32,128]{2,1,0:T(8,128)(2,1)} %get-tuple-element.7), calls=%async_computation | async-start | bytes 2097152 | tf_op jit(solution)/shard_map/all_to_all | solution.py:341
  47.6 15.8 %copy-start.5 = (bf16[128,128]{1,0:T(8,128)(2,1)S(1)}, bf16[128,128]{1,0:T(8,128)(2,1)}, u32[]{:S(2)}) copy-start(bf16[128,128]{1,0:T(8,128)(2,1)} %match.3) | copy-start | bytes 98308
  72.1 19.5 %copy-start.1 = (bf16[128,512]{1,0:T(8,128)(2,1)S(1)}, bf16[128,512]{1,0:T(8,128)(2,1)}, u32[]{:S(2)}) copy-start(bf16[128,512]{1,0:T(8,128)(2,1)} %up.1) | copy-start | bytes 393220
  72.1 19.5 %copy-start.2 = (bf16[512,128]{1,0:T(8,128)(2,1)S(1)}, bf16[512,128]{1,0:T(8,128)(2,1)}, u32[]{:S(2)}) copy-start(bf16[512,128]{1,0:T(8,128)(2,1)} %down.1) | copy-start | bytes 393220
  72.1 19.5 %copy-start.6 = (bf16[128,128]{1,0:T(8,128)(2,1)S(1)}, bf16[128,128]{1,0:T(8,128)(2,1)}, u32[]{:S(2)}) copy-start(bf16[128,128]{1,0:T(8,128)(2,1)} %out_w.3) | copy-start | bytes 98308
  91.6 0.7 copy-start.7

commit v3 on v1

v3 whole, which is shorter than its diff:
```python
import functools
import math

import jax
import jax.numpy as jnp
from jax import lax
from jax.experimental import pallas as pl
from jax.experimental.pallas import tpu as pltpu
from jax.sharding import PartitionSpec as P

HEADS = 4
HALO = 64
CHUNKS = 1
UNIT_BINS = 4
F32 = jnp.float32
BF16 = jnp.bfloat16
NEG = -1e30
ONES_ROWS = 16


def layer_norm(values, gain):
    widened = values.astype(F32)
    centred = widened - jnp.mean(widened, -1, keepdims=True)
    spread = jnp.mean(centred * centred, -1, keepdims=True)
    return (centred * lax.rsqrt(spread + 1e-05) * gain).astype(BF16)


def dot_nt(a, b):
    return lax.dot_general(a, b, (((1,), (1,)), ((), ())), preferred_element_type=F32)


def dot_tn(a, b):
    return lax.dot_general(a, b, (((0,), (0,)), ((), ())), preferred_element_type=F32)


def dot_nn(a, b):
    return jnp.dot(a, b, preferred_element_type=F32)


def query_sides(rows):
    width = rows.shape[1]
    wide = rows.astype(F32)
    head = lax.broadcasted_iota(jnp.int32, (1, width), 1) // (width // HEADS)
    scale = (width // HEADS) ** (-0.5) * math.log2(math.e)
    return jnp.concatenate(
        [(wide * jnp.where(head == h, scale, 0.0).astype(F32)).astype(BF16) for h in range(HEADS)], 0
    )


def head_pairs(values_t, weights):
    depth = values_t.shape[0] // HEADS
    columns = weights.shape[1] // HEADS
    ones = jnp.ones((ONES_ROWS, values_t.shape[1]), BF16)
    for p in range(HEADS // 2):
        low, high = 2 * p * depth, 2 * (p + 1) * depth
        found = dot_nn(
            jnp.concatenate([values_t[low:high], ones], 0), weights[:, 2 * p * columns : 2 * (p + 1) * columns]
        )
        for j in range(2):
            side = slice(j * columns, (j + 1) * columns)
            yield 2 * p + j, found[j * depth : (j + 1) * depth, side], found[2 * depth : 2 * depth + 1, side]


def pipelined(units, stages):
    count = len(stages)

    def run(u, first, last):
        for s in reversed(range(first, last)):
            stages[s](u - s)

    def step(u, carry):
        run(u, 0, count)
        return carry

    for u in range(count - 1):
        run(u, 0, u + 1)
    lax.fori_loop(count - 1, units, step, 0)
    for u in range(units, units + count - 1):
        run(u, u - units + 1, count)


def both(*stages):
    def run(u):
        for stage in stages:
            stage(u)

    return run


def project_rows(joined, match, value_t, keys, values, first, span):
    width = joined.shape[1]
    some = joined.shape[0] // span
    keys[pl.ds(first, some)] = dot_nn(joined, match[...]).astype(BF16).reshape(some, span, width)
    found = dot_nt(value_t[...], joined).astype(BF16)
    for j in range(some):
        values[first + j] = found[:, j * span : (j + 1) * span]


def own_kernel(own, bias, gain, match, value_t, keys, part_mix, part_max, part_sum, values, scores, weights):
    bins, count, width = own.shape
    depth = width // HEADS

    def project(u):
        first = u * UNIT_BINS
        rows = own[pl.ds(first, UNIT_BINS)].reshape(UNIT_BINS * count, width)
        project_rows(layer_norm(rows, gain[...]), match, value_t, keys, values, first, count)

    def score(u):
        for j in range(UNIT_BINS):
            b = u * UNIT_BINS + j
            found = dot_nt(keys[b], query_sides(keys[b])) + jnp.concatenate([bias[...]] * HEADS, 1)
            scores[j] = found
            part_max[b] = jnp.max(found, 0, keepdims=True)

    def weigh(u):
        for j in range(UNIT_BINS):
            weights[j] = jnp.exp2(scores[j] - part_max[u * UNIT_BINS + j]).astype(BF16)

    def gather(u):
        for j in range(UNIT_BINS):
            b = u * UNIT_BINS + j
            for h, mixed, total in head_pairs(values[b], weights[j]):
                part_mix[b, h * depth : (h + 1) * depth] = mixed
                part_sum[b, :, h * count : (h + 1) * count] = total

    pipelined(bins // UNIT_BINS, [project, score, weigh, gather])


def halo_kernel(
    before, own, after, bias, gain, match, value_t, out_w, freq_gain, queries, part_mix, part_max, part_sum,
    after_time, *rest
):
    sent, (keys, values, mixes, turned, scores, weights, largest, faded) = rest[:CHUNKS], rest[CHUNKS:]
    bins, count, width = own.shape
    depth = width // HEADS
    parts = sent[0].shape[0]

    def project(u):
        first = u * UNIT_BINS
        rows = []
        for j in range(UNIT_BINS):
            rows += [before[first + j], after[first + j]]
        normed = layer_norm(jnp.concatenate(rows, 0), gain[...])
        project_rows(normed, match, value_t, keys, values, first, 2 * HALO)

    def score(u):
        for j in range(UNIT_BINS):
            b = u * UNIT_BINS + j
            found = dot_nt(keys[b], query_sides(queries[b])) + jnp.concatenate([bias[...]] * HEADS, 1)
            scores[j] = found
            largest[j] = jnp.maximum(jnp.max(found, 0, keepdims=True), part_max[b])

    def weigh(u):
        for j in range(UNIT_BINS):
            weights[j] = jnp.exp2(scores[j] - largest[j]).astype(BF16)
            faded[j] = jnp.exp2(part_max[u * UNIT_BINS + j] - largest[j])

    def gather(u):
        for j in range(UNIT_BINS):
            b = u * UNIT_BINS + j
            for h, mixed, total in head_pairs(values[b], weights[j]):
                columns = slice(h * count, (h + 1) * count)
                fade = faded[j, :, columns]
                mixed = mixed + part_mix[b, h * depth : (h + 1) * depth] * fade
                total = total + part_sum[b, :, columns] * fade
                mixes[j, h * depth : (h + 1) * depth] = (mixed * (1.0 / total)).astype(BF16)

    def finish(u):
        first = u * UNIT_BINS
        found = [dot_tn(mixes[j], out_w[...]) for j in range(UNIT_BINS)]
        spec = own[pl.ds(first, UNIT_BINS)].astype(F32).reshape(UNIT_BINS * count, width)
        result = (spec + jnp.concatenate(found, 0)).astype(BF16)
        after_time[pl.ds(first, UNIT_BINS)] = result.reshape(UNIT_BINS, count, width)
        normed = layer_norm(result, freq_gain[...]).astype(F32)
        for j in range(UNIT_BINS):
            turned[pl.ds(first + j, count, stride=bins), :] = normed[j * count : (j + 1) * count]

    pipelined(bins // UNIT_BINS, [project, score, both(weigh, gather), finish])
    each = count // parts // CHUNKS

    def turn(d, carry):
        for c in range(CHUNKS):
            found = turned[pl.ds((c * parts + d) * each * bins, each * bins), :]
            sent[c][d] = found.astype(BF16).reshape(each, bins, width)
        return carry

    lax.fori_loop(0, parts, turn, 0)


def freq_kernel(rows, match, value_t, mixed_out, keys, values, scores, weights, largest):
    parts, frames, each, width = rows.shape
    bins = parts * each
    depth = width // HEADS

    def project(f):
        project_rows(rows[:, f].reshape(bins, width), match, value_t, keys, values, f, bins)

    def score(f):
        found = dot_nt(query_sides(keys[f]), keys[f])
        scores[...] = found
        for h in range(HEADS):
            largest[h : h + 1] = jnp.max(found[h * bins : (h + 1) * bins], 0, keepdims=True)

    def weigh(f):
        for h in range(HEADS):
            part = slice(h * bins, (h + 1) * bins)
            weights[part] = jnp.exp2(scores[part] - largest[h : h + 1]).astype(BF16)

    def gather(f):
        pieces = []
        ones = jnp.ones((ONES_ROWS, bins), BF16)
        for h in range(HEADS):
            own = jnp.concatenate([values[f, h * depth : (h + 1) * depth], ones], 0)
            found = dot_nn(own, weights[h * bins : (h + 1) * bins])
            pieces.append(found[:depth] * (1.0 / found[depth : depth + 1]))
        mixed_out[:, f] = jnp.concatenate(pieces, 0).T.astype(BF16).reshape(parts, each, width)

    pipelined(frames, [project, score, weigh, gather])


def full(array):
    return pl.BlockSpec(array.shape, lambda i: (0,) * len(array.shape))


def block(shape, *index):
    return pl.BlockSpec(shape, lambda i: index)


def call(kernel, name, us, **kwargs):
    return pl.pallas_call(
        kernel,
        grid=(1,),
        compiler_params=pltpu.CompilerParams(
            dimension_semantics=("arbitrary",), vmem_limit_bytes=14 << 20
        ),
        cost_estimate=pl.CostEstimate(flops=int(us * 5e8), bytes_accessed=1 << 20, transcendentals=0),
        name=name,
        **kwargs,
    )


def own_stage(spec, bias, gain, match, value_t):
    bins, count, width = spec.shape
    columns = HEADS * count
    args = (spec, bias, gain, match, value_t)
    outs = [
        jax.ShapeDtypeStruct((bins, count, width), BF16),
        jax.ShapeDtypeStruct((bins, width, count), F32),
        jax.ShapeDtypeStruct((bins, 1, columns), F32),
        jax.ShapeDtypeStruct((bins, 1, columns), F32),
    ]
    return call(
        own_kernel,
        "own_stage",
        8,
        in_specs=[full(a) for a in args],
        out_specs=[full(o) for o in outs],
        out_shape=outs,
        scratch_shapes=[
            pltpu.VMEM((bins, width, count), BF16),
            pltpu.VMEM((UNIT_BINS, count, columns), F32),
            pltpu.VMEM((UNIT_BINS, count, columns), BF16),
        ],
    )(*args)


def halo_stage(parts, before, spec, after, bias, gain, match, value_t, out_w, freq_gain, partial):
    bins, count, width = spec.shape
    columns = HEADS * count
    args = (before, spec, after, bias, gain, match, value_t, out_w, freq_gain, *partial)
    outs = [jax.ShapeDtypeStruct((bins, count, width), BF16)] + [
        jax.ShapeDtypeStruct((parts, count // parts // CHUNKS, bins, width), BF16)
    ] * CHUNKS
    return call(
        halo_kernel,
        "halo_stage",
        7,
        in_specs=[full(a) for a in args],
        out_specs=[full(o) for o in outs],
        out_shape=outs,
        scratch_shapes=[
            pltpu.VMEM((bins, 2 * HALO, width), BF16),
            pltpu.VMEM((bins, width, 2 * HALO), BF16),
            pltpu.VMEM((UNIT_BINS, width, count), BF16),
            pltpu.VMEM((count * bins, width), F32),
            pltpu.VMEM((UNIT_BINS, 2 * HALO, columns), F32),
            pltpu.VMEM((UNIT_BINS, 2 * HALO, columns), BF16),
            pltpu.VMEM((UNIT_BINS, 1, columns), F32),
            pltpu.VMEM((UNIT_BINS, 1, columns), F32),
        ],
    )(*args)


def freq_stage(rows, match, value_t):
    parts, frames, each, width = rows.shape
    bins = parts * each
    return call(
        freq_kernel,
        "freq_stage",
        5,
        in_specs=[full(rows), full(match), full(value_t)],
        out_specs=full(rows),
        out_shape=jax.ShapeDtypeStruct(rows.shape, BF16),
        scratch_shapes=[
            pltpu.VMEM((frames, bins, width), BF16),
            pltpu.VMEM((frames, width, bins), BF16),
            pltpu.VMEM((HEADS * bins, bins), F32),
            pltpu.VMEM((HEADS * bins, bins), BF16),
            pltpu.VMEM((HEADS, bins), F32),
        ],
    )(rows, match, value_t)


def add_branch(base, mixed, weight):
    return (base.astype(F32) + dot_nn(mixed, weight)).astype(BF16)


def feed_forward(after_freq, mlp_gain, mlp_up, mlp_down):
    hidden = jax.nn.gelu(dot_nn(layer_norm(after_freq, mlp_gain), mlp_up)).astype(BF16)
    return add_branch(after_freq, hidden, mlp_down)


def key_bias(segment_ids, active, count):
    frames = segment_ids.shape[0]
    span = count + 2 * HALO
    start = lax.axis_index("tm") * count
    seg_query = lax.dynamic_slice_in_dim(segment_ids, start, count, 0)
    seg_key = lax.dynamic_slice_in_dim(jnp.pad(segment_ids, HALO, constant_values=-1), start, span, 0)
    act_key = lax.dynamic_slice_in_dim(jnp.pad(active, HALO), start, span, 0)
    pos_key = start - HALO + jnp.arange(span, dtype=jnp.int32)
    pos_query = start + jnp.arange(count, dtype=jnp.int32)
    inside = (pos_key >= 0) & (pos_key < frames)
    allowed = (
        inside[:, None]
        & (seg_query[None, :] == seg_key[:, None])
        & ((act_key[:, None] == 1) | (pos_query[None, :] == pos_key[:, None]))
    )
    return jnp.where(allowed, 0.0, NEG).astype(F32)


def per_device(
    spec,
    segment_ids,
    active,
    time_gain,
    time_match,
    time_value,
    time_out,
    freq_gain,
    freq_match,
    freq_value,
    freq_out,
    mlp_gain,
    mlp_up,
    mlp_down,
):
    bins, count, width = spec.shape
    peers = lax.axis_size("tm")
    parts = lax.axis_size("freq")
    up = [(i, i + 1) for i in range(peers - 1)]
    down = [(j, i) for i, j in up]
    before = lax.ppermute(spec[:, count - HALO :], "tm", up)
    after = lax.ppermute(spec[:, :HALO], "tm", down)
    bias = key_bias(segment_ids, active, count)
    side_bias = jnp.concatenate([bias[:HALO], bias[HALO + count :]], 0)
    time_value_t, freq_value_t = time_value.T, freq_value.T
    partial = own_stage(spec, bias[HALO : HALO + count], time_gain[None], time_match, time_value_t)
    base, *sent = halo_stage(
        parts, before, spec, after, side_bias, time_gain[None], time_match, time_value_t, time_out, freq_gain[None],
        partial,
    )
    base, *sent = lax.optimization_barrier((jnp.swapaxes(base, 0, 1), *sent))
    gathered = [exchange(s) for s in sent]
    returned = [exchange(freq_stage(g, freq_match, freq_value_t)) for g in gathered]
    mixed = returned[0].reshape(count, bins, width)
    after_freq = add_branch(base, mixed, freq_out)
    result = lax.optimization_barrier(feed_forward(after_freq, mlp_gain, mlp_up, mlp_down))
    return jnp.swapaxes(result, 0, 1)


def exchange(array):
    return lax.all_to_all(array, "freq", split_axis=0, concat_axis=0, tiled=True)


def solution(mesh):
    placed = (P("freq", "tm", None),) + (P(),) * 13
    return jax.shard_map(
        per_device, mesh=mesh, in_specs=placed, out_specs=P("freq", "tm", None), check_vma=False
    )
```

time: 160 us -> 85.8 us (0.54)
  Pallas kernels: 96.4 us -> 20.2 us
  matrix products: 0 us -> 5.05 us
  waiting for transfers between devices: 26.7 us -> 22.7 us
  other arithmetic: 0.38 us -> 2.33 us
    pallas_call x3, Pallas kernels: 96.4 us -> 20.2 us  [the longest x1 8.51 us: halo_stage(): call(halo_kernel, 'halo_stage', 7, in_specs=[full(a) for a in args], out_...]
    dot_general x0 -> x2, matrix products: none -> 5.05 us  [dot_nn(): return jnp.dot(a, b, preferred_element_type=F32)]
    ppermute x1, waiting for transfers between devices: 6.39 us -> 2.67 us  [per_device(): before = lax.ppermute(spec[:, count - HALO:], 'tm', up)]
    reduce_sum x0 -> x2, other arithmetic: none -> 1.93 us  [the longest x1 1.29 us: layer_norm(): spread = jnp.mean(centred * centred, -1, keepdims=True)]
    unnamed x30, local copies, waits for them, and re-layouts: 2.2 us -> 0.29 us
  transfers between devices with their start and end apart: 3 -> 3, of which waited for: 3 -> 3; matrix products, arithmetic and copies ran while one was open for 0% -> 1% of each run, Pallas kernels for 0% -> 5%
where the time goes in v3:
time: 85.8 us; the launch traced here: 85.4 us
  waiting for transfers between devices  22.7 us (26%)
  Pallas kernels  20.2 us (24%)
  blocking collectives  19.4 us (23%)
  starting transfers between devices  13 us (15%)
  matrix products  5.05 us (6%)
  local copies, waits for them, and re-layouts  2.54 us (3%)
  other arithmetic  2.33 us (3%)
    all_to_all x1, blocking collectives, exchange(): lax.all_to_all(array, 'freq', split_axis=0, concat_axis=0, tiled=True)  19.4 us
    all_to_all x1, waiting for transfers between devices, exchange(): lax.all_to_all(array, 'freq', split_axis=0, concat_axis=0, tiled=True)  15.6 us
    pallas_call x1, Pallas kernels, halo_stage(): call(halo_kernel, 'halo_stage', 7, in_specs=[full(a) for a in args], out_...  8.51 us
    pallas_call x1, Pallas kernels, freq_stage(): call(freq_kernel, 'freq_stage', 5, in_specs=[full(rows), full(match), ful...  7.15 us
    ppermute x1, starting transfers between devices, per_device(): after = lax.ppermute(spec[:, :HALO], 'tm', down)  6.65 us
    dot_general x2, matrix products, dot_nn(): return jnp.dot(a, b, preferred_element_type=F32)  5.05 us
    pallas_call x1, Pallas kernels, own_stage(): call(own_kernel, 'own_stage', 8, in_specs=[full(a) for a in args], out_sp...  4.49 us
    all_to_all x1, starting transfers between devices, exchange(): lax.all_to_all(array, 'freq', split_axis=0, concat_axis=0, tiled=True)  4.42 us
  transfers between devices with their start and end apart: 3, of which 3 were waited for; matrix products, arithmetic and copies ran while one was open for 1% of the time, Pallas kernels for 5%

profile of v3, /device:TPU:448, one launch (start us, length us, event | category | flops | bytes accessed | tf_op | source)
XLA Modules:
  0.0 85.4 jit_solution(1072212647144826619)
XLA Ops:
  0.0 0.0 copy-start
  0.0 0.0 copy-start.1
  0.0 0.0 copy-start.9
  0.0 0.0 copy-start.8
  0.0 0.0 copy-start.10
  0.0 0.0 copy-start.5
  0.0 0.0 copy-start.2
  0.1 2.2 %fusion.39 = (bf16[32,64,128]{2,1,0:T(8,128)(2,1)S(1)}, bf16[32,64,128]{2,1,0:T(8,128)(2,1)}) fusion(bf16[32,128,128]{2,1,0:T(8,128)(2,1)} %own.3), kind=kLoop, calls=%fused_computation.43 | loop fusion | bytes 2097152 | tf_op jit(solution)/shard_map/slice | solution.py:363
  2.2 1.9 %collective-permute-start = (bf16[32,64,128]{2,1,0:T(8,128)(2,1)}, bf16[32,64,128]{2,1,0:T(8,128)(2,1)S(1)}, u32[]{:S(2)}, u32[]{:S(2)}) collective-permute-start(bf16[32,64,128]{2,1,0:T(8,128)(2,1)} %get-tuple-element.24), channel_id=1, source_target_pairs={{0,8},{8,16},{16,24},{24,32},{32,40},{40,48},{48,56},{56,64},{64,7... | collective-permute-start | bytes 1572872 | tf_op jit(solution)/shard_map/ppermute | solution.py:362
  4.1 6.7 %collective-permute-start.1 = (bf16[32,64,128]{2,1,0:T(8,128)(2,1)S(1)}, bf16[32,64,128]{2,1,0:T(8,128)(2,1)S(1)}, u32[]{:S(2)}, u32[]{:S(2)}) collective-permute-start(bf16[32,64,128]{2,1,0:T(8,128)(2,1)S(1)} %get-tuple-element.23), channel_id=1, source_target_pairs={{8,0},{16,8},{24,16},{32,24},{40,32},{48,40},{56,48},{64,56},{72,6... | collective-permute-start | bytes 1572872 | tf_op jit(solution)/shard_map/ppermute | solution.py:363
  10.8 0.0 copy-done.9
  10.8 0.1 pad_dynamic-slice_fusion.1
  10.9 0.0 copy-done.8
  10.9 0.1 compare_and_fusion
  11.0 0.1 dynamic_slice.9
  11.1 0.2 and_select_fusion
  11.3 0.0 copy-done.10
  11.3 0.1 copy.15
  11.4 0.0 copy-done.1
  11.4 0.0 copy-done.5
  11.5 0.0 copy-done.2
  11.5 0.0 copy-start.3
  11.5 0.0 copy-start.6
  11.5 4.5 %own_stage.1 = (bf16[32,128,128]{2,1,0:T(8,128)(2,1)S(1)}, f32[32,128,128]{2,1,0:T(8,128)S(1)}, f32[32,1,512]{2,1,0:T(1,128)S(1)}, f32[32,1,512]{2,1,0:T(1,128)S(1)}) custom-call(bf16[32,128,128]{2,1,0:T(8,128)(2,1)S(1)} %copy-done.1, f32[128,128]{1,0:T(8,128)S(1)} %slice.22.bias, f32[1,128]{1,0:T(1,128)S(1)} %bitcast.21, bf16[128,128]{1,0:T(8,128)(2,1)S(1)} %copy-done.2, ...), custom_call_target="tpu_custom_call" | custom-call | flops 4000000000 | bytes 1048576 | tf_op jit(solution)/shard_map/own_stage/pallas_call | solution.py:252
  16.0 2.7 %collective-permute-done.before = bf16[32,64,128]{2,1,0:T(8,128)(2,1)S(1)} collective-permute-done((bf16[32,64,128]{2,1,0:T(8,128)(2,1)}, bf16[32,64,128]{2,1,0:T(8,128)(2,1)S(1)}, u32[]{:S(2)}, u32[]{:S(2)}) %collective-permute-start) | collective-permute-done | bytes 524320 | tf_op jit(solution)/shard_map/ppermute | solution.py:362
  18.7 4.4 %collective-permute-done.1.after = bf16[32,64,128]{2,1,0:T(8,128)(2,1)S(1)} collective-permute-done((bf16[32,64,128]{2,1,0:T(8,128)(2,1)S(1)}, bf16[32,64,128]{2,1,0:T(8,128)(2,1)S(1)}, u32[]{:S(2)}, u32[]{:S(2)}) %collective-permute-start.1) | collective-permute-done | bytes 524320 | tf_op jit(solution)/shard_map/ppermute | solution.py:363
  23.1 0.0 copy-done.3
  23.1 0.0 copy-done.6
  23.1 8.5 %halo_stage.1 = (bf16[32,128,128]{2,1,0:T(8,128)(2,1)S(1)}, bf16[8,16,32,128]{3,2,1,0:T(8,128)(2,1)}) custom-call(bf16[32,64,128]{2,1,0:T(8,128)(2,1)S(1)} %collective-permute-done.before, bf16[32,128,128]{2,1,0:T(8,128)(2,1)S(1)} %copy-done.1, bf16[32,64,128]{2,1,0:T(8,128)(2,1)S(1)} %collective-permute-done.1.after, f32[128,128]{1,0:T(8,128)S(1)} %pad_maximum_fusion.bias, ...), custom_call_target="tpu_custom_call" | custom-call | flops 3500000000 | bytes 1048576 | tf_op jit(solution)/shard_map/halo_stage/pallas_call | solution.py:274
  31.6 0.0 copy-start.11
  31.6 4.4 %all-to-all-start = ((bf16[8,16,32,128]{3,2,1,0:T(8,128)(2,1)}), bf16[8,16,32,128]{3,2,1,0:T(8,128)(2,1)S(1)}, u32[]{:S(2)}, u32[]{:S(2)}) async-start(bf16[8,16,32,128]{3,2,1,0:T(8,128)(2,1)} %get-tuple-element.20), calls=%async_computation | async-start | bytes 2097152 | tf_op jit(solution)/shard_map/all_to_all | solution.py:382
  36.0 0.0 copy-done.11
  36.0 0.1 copy.16
  36.1 15.6 %all-to-all-done.rows = bf16[8,16,32,128]{3,2,1,0:T(8,128)(2,1)S(1)} async-done(((bf16[8,16,32,128]{3,2,1,0:T(8,128)(2,1)}), bf16[8,16,32,128]{3,2,1,0:T(8,128)(2,1)S(1)}, u32[]{:S(2)}, u32[]{:S(2)}) %all-to-all-start) | async-done | bytes 1048608 | tf_op jit(solution)/shard_map/all_to_all | solution.py:382
  51.8 0.0 copy-done.4
  51.8 7.2 %freq_stage.1 = bf16[8,16,32,128]{3,2,1,0:T(8,128)(2,1)S(1)} custom-call(bf16[8,16,32,128]{3,2,1,0:T(8,128)(2,1)S(1)} %all-to-all-done.rows, bf16[128,128]{1,0:T(8,128)(2,1)S(1)} %copy-done.4, bf16[128,128]{1,0:T(8,128)(2,1)S(1)} %bitcast.20), custom_call_target="tpu_custom_call" | custom-call | flops 2500000000 | bytes 1048576 | tf_op jit(solution)/shard_map/freq_stage/pallas_call | solution.py:297
  59.0 0.0 copy-start.7
  59.0 19.4 %all_to_all.10 = bf16[8,16,32,128]{3,2,1,0:T(8,128)(2,1)S(1)} all-to-all(bf16[8,16,32,128]{3,2,1,0:T(8,128)(2,1)S(1)} %freq_stage.1), channel_id=1, replica_groups=mesh['tm'=64,'freq'=8] {'freq'}, dimensions={0} | all-to-all | bytes 2097152 | tf_op jit(solution)/shard_map/all_to_all | solution.py:382
  78.3 0.0 copy-done.7
  78.3 0.5 fusion.22
  78.9 0.0 copy-start.12
  78.9 0.0 copy-start.13
  78.9 0.6 convert_reduce_fusion
  79.5 1.3 %fusion.14 = f32[128,32]{0,1:T(8,128)S(1)} fusion(bf16[128,32,128]{2,0,1:T(8,128)(2,1)S(1)} %get-tuple-element.22, f32[128,32]{0,1:T(8,128)S(1)} %broadcast_multiply_fusion), kind=kLoop, calls=%fused_computation.16 | loop fusion | flops 2093056 | bytes 1081344 | tf_op jit(solution)/shard_map/reduce_sum | solution.py:24
  80.9 0.0 copy-done
  80.9 0.0 copy-done.12
  80.9 0.0 copy-done.13
  80.9 4.5 %fusion.17 = bf16[128,32,128]{2,0,1:T(8,128)(2,1)} fusion(bf16[128,32,128]{2,0,1:T(8,128)(2,1)S(1)} %get-tuple-element.22, f32[128]{0:T(128)S(1)} %copy-done.13, f32[128,32]{0,1:T(8,128)S(1)} %add_rsqrt_fusion, f32[128,32]{0,1:T(8,128)S(1)} %broadcast_multiply_fusion, bf16[512,128]{1,0:T(8,128)(2,1)S(1)} %copy-done, bf16[128,512]{1,0:T(8,128)(2,1)S(1)} %copy-done.12), kind=kOutput, calls=%fused_computation.19 | convolution fusion | flops 1096810496 | bytes 2392576 | tf_op jit(solution)/shard_map/dot_general | solution.py:37
  (7 shorter events, 0.0 us)
Async XLA Ops:
  0.0 80.9 %copy-start = (bf16[512,128]{1,0:T(8,128)(2,1)S(1)}, bf16[512,128]{1,0:T(8,128)(2,1)}, u32[]{:S(2)}) copy-start(bf16[512,128]{1,0:T(8,128)(2,1)} %param.27) | copy-start | bytes 393220
  0.0 11.4 %copy-start.1 = (bf16[32,128,128]{2,1,0:T(8,128)(2,1)S(1)}, bf16[32,128,128]{2,1,0:T(8,128)(2,1)}, u32[]{:S(2)}) copy-start(bf16[32,128,128]{2,1,0:T(8,128)(2,1)} %own.3) | copy-start | bytes 3145732
  0.0 10.8 %copy-start.9 = (s32[8192]{0:T(1024)S(1)}, s32[8192]{0:T(1024)}, u32[]{:S(2)}) copy-start(s32[8192]{0:T(1024)} %param.15) | copy-start | bytes 98308
  0.0 10.9 %copy-start.8 = (s32[8192]{0:T(1024)S(1)}, s32[8192]{0:T(1024)}, u32[]{:S(2)}) copy-start(s32[8192]{0:T(1024)} %param.16) | copy-start | bytes 98308
  0.0 11.3 %copy-start.10 = (bf16[128,128]{1,0:T(8,128)(2,1)S(1)}, bf16[128,128]{1,0:T(8,128)(2,1)}, u32[]{:S(2)}) copy-start(bf16[128,128]{1,0:T(8,128)(2,1)} %param.19) | copy-start | bytes 98308
  0.0 11.4 %copy-start.5 = (f32[128]{0:T(128)S(1)}, f32[128]{0:T(128)}, u32[]{:S(2)}) copy-start(f32[128]{0:T(128)} %param.17) | copy-start | bytes 1540
  0.0 11.4 %copy-start.2 = (bf16[128,128]{1,0:T(8,128)(2,1)S(1)}, bf16[128,128]{1,0:T(8,128)(2,1)}, u32[]{:S(2)}) copy-start(bf16[128,128]{1,0:T(8,128)(2,1)} %match.4) | copy-start | bytes 98308
  2.2 16.4 %collective-permute-start = (bf16[32,64,128]{2,1,0:T(8,128)(2,1)}, bf16[32,64,128]{2,1,0:T(8,128)(2,1)S(1)}, u32[]{:S(2)}, u32[]{:S(2)}) collective-permute-start(bf16[32,64,128]{2,1,0:T(8,128)(2,1)} %get-tuple-element.24), channel_id=1, source_target_pairs={{0,8},{8,16},{16,24},{24,32},{32,40},{40,48},{48,56},{56,64},{64,7... | collective-permute-start | bytes 1572872 | tf_op jit(solution)/shard_map/ppermute | solution.py:362
  4.1 19.0 %collective-permute-start.1 = (bf16[32,64,128]{2,1,0:T(8,128)(2,1)S(1)}, bf16[32,64,128]{2,1,0:T(8,128)(2,1)S(1)}, u32[]{:S(2)}, u32[]{:S(2)}) collective-permute-start(bf16[32,64,128]{2,1,0:T(8,128)(2,1)S(1)} %get-tuple-element.23), channel_id=1, source_target_pairs={{8,0},{16,8},{24,16},{32,24},{40,32},{48,40},{56,48},{64,56},{72,6... | collective-permute-start | bytes 1572872 | tf_op jit(solution)/shard_map/ppermute | solution.py:363
  11.5 11.6 %copy-start.3 = (bf16[128,128]{1,0:T(8,128)(2,1)S(1)}, bf16[128,128]{1,0:T(8,128)(2,1)}, u32[]{:S(2)}) copy-start(bf16[128,128]{1,0:T(8,128)(2,1)} %out_w.1) | copy-start | bytes 98308
  11.5 11.6 %copy-start.6 = (f32[128]{0:T(128)S(1)}, f32[128]{0:T(128)}, u32[]{:S(2)}) copy-start(f32[128]{0:T(128)} %param.21) | copy-start | bytes 1540
  31.6 4.4 %copy-start.11 = (bf16[128,128]{1,0:T(8,128)(2,1)S(1)}, bf16[128,128]{1,0:T(8,128)(2,1)}, u32[]{:S(2)}) copy-start(bf16[128,128]{1,0:T(8,128)(2,1)} %param.23) | copy-start | bytes 98308
  31.6 20.2 %copy-start.4 = (bf16[128,128]{1,0:T(8,128)(2,1)S(1)}, bf16[128,128]{1,0:T(8,128)(2,1)}, u32[]{:S(2)}) copy-start(bf16[128,128]{1,0:T(8,128)(2,1)} %match.5) | copy-start | bytes 98308
  31.6 20.2 %all-to-all-start = ((bf16[8,16,32,128]{3,2,1,0:T(8,128)(2,1)}), bf16[8,16,32,128]{3,2,1,0:T(8,128)(2,1)S(1)}, u32[]{:S(2)}, u32[]{:S(2)}) async-start(bf16[8,16,32,128]{3,2,1,0:T(8,128)(2,1)} %get-tuple-element.20), calls=%async_computation | async-start | bytes 2097152 | tf_op jit(solution)/shard_map/all_to_all | solution.py:382
  59.0 19.4 %copy-start.7 = (bf16[128,128]{1,0:T(8,128)(2,1)S(1)}, bf16[128,128]{1,0:T(8,128)(2,1)}, u32[]{:S(2)}) copy-start(bf16[128,128]{1,0:T(8,128)(2,1)} %param.24) | copy-start | bytes 98308
  78.9 2.0 %copy-start.12 = (bf16[128,512]{1,0:T(8,128)(2,1)S(1)}, bf16[128,512]{1,0:T(8,128)(2,1)}, u32[]{:S(2)}) copy-start(bf16[128,512]{1,0:T(8,128)(2,1)} %param.26) | copy-start | bytes 393220
  78.9 2.0 %copy-start.13 = (f32[128]{0:T(128)S(1)}, f32[128]{0:T(128)}, u32[]{:S(2)}) copy-start(f32[128]{0:T(128)} %param.25) | copy-start | bytes 1540

commit v4 on v3

--- a/solution.py
+++ b/solution.py
@@ -231,7 +231,7 @@
         kernel,
         grid=(1,),
         compiler_params=pltpu.CompilerParams(
-            dimension_semantics=("arbitrary",), vmem_limit_bytes=14 << 20
+            dimension_semantics=("arbitrary",), vmem_limit_bytes=8 << 20
         ),
         cost_estimate=pl.CostEstimate(flops=int(us * 5e8), bytes_accessed=1 << 20, transcendentals=0),
         name=name,
@@ -369,7 +369,7 @@
         parts, before, spec, after, side_bias, time_gain[None], time_match, time_value_t, time_out, freq_gain[None],
         partial,
     )
-    base, *sent = lax.optimization_barrier((jnp.swapaxes(base, 0, 1), *sent))
+    base, freq_value_t, *sent = lax.optimization_barrier((jnp.swapaxes(base, 0, 1), freq_value_t, *sent))
     gathered = [exchange(s) for s in sent]
     returned = [exchange(freq_stage(g, freq_match, freq_value_t)) for g in gathered]
     mixed = returned[0].reshape(count, bins, width)

time: 85.8 us -> 83.7 us (0.976)
  blocking collectives: 19.4 us -> 39.2 us
  waiting for transfers between devices: 22.7 us -> 6.96 us
  starting transfers between devices: 13 us -> 8.57 us
  Pallas kernels: 20.2 us -> 19.2 us
    all_to_all x1 -> x2, blocking collectives: 19.4 us -> 39.2 us  [exchange(): lax.all_to_all(array, 'freq', split_axis=0, concat_axis=0, tiled=True)]
    all_to_all x1 -> x0, waiting for transfers between devices: 15.6 us -> none  [exchange(): lax.all_to_all(array, 'freq', split_axis=0, concat_axis=0, tiled=True)]
    all_to_all x1 -> x0, starting transfers between devices: 4.42 us -> none  [exchange(): lax.all_to_all(array, 'freq', split_axis=0, concat_axis=0, tiled=True)]
    pallas_call x1, Pallas kernels: 8.51 us -> 7.55 us  [halo_stage(): call(halo_kernel, 'halo_stage', 7, in_specs=[full(a) for a in args], out_...]
  transfers between devices with their start and end apart: 3 -> 2, of which waited for: 3 -> 2; matrix products, arithmetic and copies ran while one was open for 1% -> 1% of each run, Pallas kernels for 5% -> 5%
where the time goes in v4:
time: 83.7 us; the launch traced here: 83.4 us
  blocking collectives  39.2 us (47%)
  Pallas kernels  19.2 us (23%)
  starting transfers between devices  8.57 us (10%)
  waiting for transfers between devices  6.96 us (8%)
  matrix products  5.05 us (6%)
  other arithmetic  2.31 us (3%)
  local copies, waits for them, and re-layouts  1.75 us (2%)
    all_to_all x2, blocking collectives, exchange(): lax.all_to_all(array, 'freq', split_axis=0, concat_axis=0, tiled=True)  39.2 us
    pallas_call x1, Pallas kernels, halo_stage(): call(halo_kernel, 'halo_stage', 7, in_specs=[full(a) for a in args], out_...  7.55 us
    pallas_call x1, Pallas kernels, freq_stage(): call(freq_kernel, 'freq_stage', 5, in_specs=[full(rows), full(match), ful...  7.15 us
    ppermute x1, starting transfers between devices, per_device(): after = lax.ppermute(spec[:, :HALO], 'tm', down)  6.65 us
    dot_general x2, matrix products, dot_nn(): return jnp.dot(a, b, preferred_element_type=F32)  5.05 us
    ppermute x1, waiting for transfers between devices, per_device(): after = lax.ppermute(spec[:, :HALO], 'tm', down)  4.63 us
    pallas_call x1, Pallas kernels, own_stage(): call(own_kernel, 'own_stage', 8, in_specs=[full(a) for a in args], out_sp...  4.49 us
    ppermute x1, waiting for transfers between devices, per_device(): before = lax.ppermute(spec[:, count - HALO:], 'tm', up)  2.33 us
  transfers between devices with their start and end apart: 2, of which 2 were waited for; matrix products, arithmetic and copies ran while one was open for 1% of the time, Pallas kernels for 5%

profile of v4, /device:TPU:448, one launch (start us, length us, event | category | flops | bytes accessed | tf_op | source)
XLA Modules:
  0.0 83.4 jit_solution(2598881840583402072)
XLA Ops:
  0.0 0.0 copy-start
  0.0 0.0 copy-start.1
  0.0 0.0 copy-start.9
  0.0 0.0 copy-start.8
  0.0 0.0 copy-start.10
  0.0 0.0 copy-start.11
  0.0 0.0 copy-start.5
  0.1 0.0 copy-start.2
  0.1 1.4 %fusion.39 = (bf16[32,64,128]{2,1,0:T(8,128)(2,1)S(1)}, bf16[32,64,128]{2,1,0:T(8,128)(2,1)S(1)}) fusion(bf16[32,128,128]{2,1,0:T(8,128)(2,1)} %own.3), kind=kLoop, calls=%fused_computation.43 | loop fusion | bytes 2097152 | tf_op jit(solution)/shard_map/slice | solution.py:363
  1.4 1.9 %collective-permute-start = (bf16[32,64,128]{2,1,0:T(8,128)(2,1)S(1)}, bf16[32,64,128]{2,1,0:T(8,128)(2,1)S(1)}, u32[]{:S(2)}, u32[]{:S(2)}) collective-permute-start(bf16[32,64,128]{2,1,0:T(8,128)(2,1)S(1)} %get-tuple-element.26), channel_id=1, source_target_pairs={{0,8},{8,16},{16,24},{24,32},{32,40},{40,48},{48,56},{56,64},{64,7... | collective-permute-start | bytes 1572872 | tf_op jit(solution)/shard_map/ppermute | solution.py:362
  3.4 6.7 %collective-permute-start.1 = (bf16[32,64,128]{2,1,0:T(8,128)(2,1)S(1)}, bf16[32,64,128]{2,1,0:T(8,128)(2,1)S(1)}, u32[]{:S(2)}, u32[]{:S(2)}) collective-permute-start(bf16[32,64,128]{2,1,0:T(8,128)(2,1)S(1)} %get-tuple-element.25), channel_id=1, source_target_pairs={{8,0},{16,8},{24,16},{32,24},{40,32},{48,40},{56,48},{64,56},{72,6... | collective-permute-start | bytes 1572872 | tf_op jit(solution)/shard_map/ppermute | solution.py:363
  10.0 0.0 copy-done.9
  10.0 0.1 pad_dynamic-slice_fusion.1
  10.1 0.0 copy-done.8
  10.1 0.1 compare_and_fusion
  10.2 0.1 dynamic_slice.9
  10.3 0.2 and_select_fusion
  10.5 0.0 copy-done.10
  10.5 0.1 copy.15
  10.7 0.0 copy-done.11
  10.7 0.1 copy.16
  10.8 0.0 copy-done.1
  10.8 0.0 copy-done.5
  10.8 0.0 copy-done.2
  10.8 0.0 copy-start.3
  10.8 0.0 copy-start.6
  10.9 4.5 %own_stage.1 = (bf16[32,128,128]{2,1,0:T(8,128)(2,1)S(1)}, f32[32,128,128]{2,1,0:T(8,128)S(1)}, f32[32,1,512]{2,1,0:T(1,128)S(1)}, f32[32,1,512]{2,1,0:T(1,128)S(1)}) custom-call(bf16[32,128,128]{2,1,0:T(8,128)(2,1)S(1)} %copy-done.1, f32[128,128]{1,0:T(8,128)S(1)} %slice.22.bias, f32[1,128]{1,0:T(1,128)S(1)} %bitcast.21, bf16[128,128]{1,0:T(8,128)(2,1)S(1)} %copy-done.2, ...), custom_call_target="tpu_custom_call" | custom-call | flops 4000000000 | bytes 1048576 | tf_op jit(solution)/shard_map/own_stage/pallas_call | solution.py:252
  15.3 2.3 %collective-permute-done.before = bf16[32,64,128]{2,1,0:T(8,128)(2,1)S(1)} collective-permute-done((bf16[32,64,128]{2,1,0:T(8,128)(2,1)S(1)}, bf16[32,64,128]{2,1,0:T(8,128)(2,1)S(1)}, u32[]{:S(2)}, u32[]{:S(2)}) %collective-permute-start) | collective-permute-done | bytes 524320 | tf_op jit(solution)/shard_map/ppermute | solution.py:362
  17.7 4.6 %collective-permute-done.1.after = bf16[32,64,128]{2,1,0:T(8,128)(2,1)S(1)} collective-permute-done((bf16[32,64,128]{2,1,0:T(8,128)(2,1)S(1)}, bf16[32,64,128]{2,1,0:T(8,128)(2,1)S(1)}, u32[]{:S(2)}, u32[]{:S(2)}) %collective-permute-start.1) | collective-permute-done | bytes 524320 | tf_op jit(solution)/shard_map/ppermute | solution.py:363
  22.3 0.0 copy-done.3
  22.3 0.0 copy-done.6
  22.3 7.5 %halo_stage.1 = (bf16[32,128,128]{2,1,0:T(8,128)(2,1)S(1)}, bf16[8,16,32,128]{3,2,1,0:T(8,128)(2,1)S(1)}) custom-call(bf16[32,64,128]{2,1,0:T(8,128)(2,1)S(1)} %collective-permute-done.before, bf16[32,128,128]{2,1,0:T(8,128)(2,1)S(1)} %copy-done.1, bf16[32,64,128]{2,1,0:T(8,128)(2,1)S(1)} %collective-permute-done.1.after, ...), custom_call_target="tpu_custom_call" | custom-call | flops 3500000000 | bytes 1048576 | tf_op jit(solution)/shard_map/halo_stage/pallas_call | solution.py:274
  29.9 0.0 copy-start.4
  29.9 20.5 %all_to_all.10.rows = bf16[8,16,32,128]{3,2,1,0:T(8,128)(2,1)S(1)} all-to-all(bf16[8,16,32,128]{3,2,1,0:T(8,128)(2,1)S(1)} %get-tuple-element.21), channel_id=1, replica_groups=mesh['tm'=64,'freq'=8] {'freq'}, dimensions={0} | all-to-all | bytes 2097152 | tf_op jit(solution)/shard_map/all_to_all | solution.py:382
  50.4 0.0 copy-done.4
  50.4 7.1 %freq_stage.1 = bf16[8,16,32,128]{3,2,1,0:T(8,128)(2,1)S(1)} custom-call(bf16[8,16,32,128]{3,2,1,0:T(8,128)(2,1)S(1)} %all_to_all.10.rows, bf16[128,128]{1,0:T(8,128)(2,1)S(1)} %copy-done.4, bf16[128,128]{1,0:T(8,128)(2,1)S(1)} %bitcast.18), custom_call_target="tpu_custom_call" | custom-call | flops 2500000000 | bytes 1048576 | tf_op jit(solution)/shard_map/freq_stage/pallas_call | solution.py:297
  57.5 0.0 copy-start.7
  57.5 18.8 %all_to_all.11 = bf16[8,16,32,128]{3,2,1,0:T(8,128)(2,1)S(1)} all-to-all(bf16[8,16,32,128]{3,2,1,0:T(8,128)(2,1)S(1)} %freq_stage.1), channel_id=1, replica_groups=mesh['tm'=64,'freq'=8] {'freq'}, dimensions={0} | all-to-all | bytes 2097152 | tf_op jit(solution)/shard_map/all_to_all | solution.py:382
  76.3 0.0 copy-done.7
  76.3 0.5 fusion.22
  76.8 0.0 copy-start.12
  76.8 0.0 copy-start.13
  76.8 0.6 convert_reduce_fusion
  77.5 1.3 %fusion.14 = f32[128,32]{0,1:T(8,128)S(1)} fusion(bf16[128,32,128]{2,0,1:T(8,128)(2,1)S(1)} %get-tuple-element.24, f32[128,32]{0,1:T(8,128)S(1)} %broadcast_multiply_fusion), kind=kLoop, calls=%fused_computation.16 | loop fusion | flops 2093056 | bytes 1081344 | tf_op jit(solution)/shard_map/reduce_sum | solution.py:24
  78.8 0.0 copy-done
  78.8 0.0 copy-done.12
  78.8 0.0 copy-done.13
  78.8 4.5 %fusion.17 = bf16[128,32,128]{2,0,1:T(8,128)(2,1)} fusion(bf16[128,32,128]{2,0,1:T(8,128)(2,1)S(1)} %get-tuple-element.24, f32[128]{0:T(128)S(1)} %copy-done.13, f32[128,32]{0,1:T(8,128)S(1)} %add_rsqrt_fusion, f32[128,32]{0,1:T(8,128)S(1)} %broadcast_multiply_fusion, bf16[512,128]{1,0:T(8,128)(2,1)S(1)} %copy-done, bf16[128,512]{1,0:T(8,128)(2,1)S(1)} %copy-done.12), kind=kOutput, calls=%fused_computation.19 | convolution fusion | flops 1096810496 | bytes 2392576 | tf_op jit(solution)/shard_map/dot_general | solution.py:37
  (6 shorter events, 0.0 us)
Async XLA Ops:
  0.0 78.8 %copy-start = (bf16[512,128]{1,0:T(8,128)(2,1)S(1)}, bf16[512,128]{1,0:T(8,128)(2,1)}, u32[]{:S(2)}) copy-start(bf16[512,128]{1,0:T(8,128)(2,1)} %param.27) | copy-start | bytes 393220
  0.0 10.8 %copy-start.1 = (bf16[32,128,128]{2,1,0:T(8,128)(2,1)S(1)}, bf16[32,128,128]{2,1,0:T(8,128)(2,1)}, u32[]{:S(2)}) copy-start(bf16[32,128,128]{2,1,0:T(8,128)(2,1)} %own.3) | copy-start | bytes 3145732
  0.0 10.0 %copy-start.9 = (s32[8192]{0:T(1024)S(1)}, s32[8192]{0:T(1024)}, u32[]{:S(2)}) copy-start(s32[8192]{0:T(1024)} %param.15) | copy-start | bytes 98308
  0.0 10.1 %copy-start.8 = (s32[8192]{0:T(1024)S(1)}, s32[8192]{0:T(1024)}, u32[]{:S(2)}) copy-start(s32[8192]{0:T(1024)} %param.16) | copy-start | bytes 98308
  0.0 10.5 %copy-start.10 = (bf16[128,128]{1,0:T(8,128)(2,1)S(1)}, bf16[128,128]{1,0:T(8,128)(2,1)}, u32[]{:S(2)}) copy-start(bf16[128,128]{1,0:T(8,128)(2,1)} %param.19) | copy-start | bytes 98308
  0.0 10.6 %copy-start.11 = (bf16[128,128]{1,0:T(8,128)(2,1)S(1)}, bf16[128,128]{1,0:T(8,128)(2,1)}, u32[]{:S(2)}) copy-start(bf16[128,128]{1,0:T(8,128)(2,1)} %param.23) | copy-start | bytes 98308
  0.0 10.8 %copy-start.5 = (f32[128]{0:T(128)S(1)}, f32[128]{0:T(128)}, u32[]{:S(2)}) copy-start(f32[128]{0:T(128)} %param.17) | copy-start | bytes 1540
  0.1 10.8 %copy-start.2 = (bf16[128,128]{1,0:T(8,128)(2,1)S(1)}, bf16[128,128]{1,0:T(8,128)(2,1)}, u32[]{:S(2)}) copy-start(bf16[128,128]{1,0:T(8,128)(2,1)} %match.4) | copy-start | bytes 98308
  1.4 16.3 %collective-permute-start = (bf16[32,64,128]{2,1,0:T(8,128)(2,1)S(1)}, bf16[32,64,128]{2,1,0:T(8,128)(2,1)S(1)}, u32[]{:S(2)}, u32[]{:S(2)}) collective-permute-start(bf16[32,64,128]{2,1,0:T(8,128)(2,1)S(1)} %get-tuple-element.26), channel_id=1, source_target_pairs={{0,8},{8,16},{16,24},{24,32},{32,40},{40,48},{48,56},{56,64},{64,7... | collective-permute-start | bytes 1572872 | tf_op jit(solution)/shard_map/ppermute | solution.py:362
  3.4 19.0 %collective-permute-start.1 = (bf16[32,64,128]{2,1,0:T(8,128)(2,1)S(1)}, bf16[32,64,128]{2,1,0:T(8,128)(2,1)S(1)}, u32[]{:S(2)}, u32[]{:S(2)}) collective-permute-start(bf16[32,64,128]{2,1,0:T(8,128)(2,1)S(1)} %get-tuple-element.25), channel_id=1, source_target_pairs={{8,0},{16,8},{24,16},{32,24},{40,32},{48,40},{56,48},{64,56},{72,6... | collective-permute-start | bytes 1572872 | tf_op jit(solution)/shard_map/ppermute | solution.py:363
  10.8 11.5 %copy-start.3 = (bf16[128,128]{1,0:T(8,128)(2,1)S(1)}, bf16[128,128]{1,0:T(8,128)(2,1)}, u32[]{:S(2)}) copy-start(bf16[128,128]{1,0:T(8,128)(2,1)} %out_w.1) | copy-start | bytes 98308
  10.8 11.5 %copy-start.6 = (f32[128]{0:T(128)S(1)}, f32[128]{0:T(128)}, u32[]{:S(2)}) copy-start(f32[128]{0:T(128)} %param.21) | copy-start | bytes 1540
  29.9 20.5 %copy-start.4 = (bf16[128,128]{1,0:T(8,128)(2,1)S(1)}, bf16[128,128]{1,0:T(8,128)(2,1)}, u32[]{:S(2)}) copy-start(bf16[128,128]{1,0:T(8,128)(2,1)} %match.5) | copy-start | bytes 98308
  57.5 18.8 %copy-start.7 = (bf16[128,128]{1,0:T(8,128)(2,1)S(1)}, bf16[128,128]{1,0:T(8,128)(2,1)}, u32[]{:S(2)}) copy-start(bf16[128,128]{1,0:T(8,128)(2,1)} %param.24) | copy-start | bytes 98308
  76.8 2.0 %copy-start.12 = (bf16[128,512]{1,0:T(8,128)(2,1)S(1)}, bf16[128,512]{1,0:T(8,128)(2,1)}, u32[]{:S(2)}) copy-start(bf16[128,512]{1,0:T(8,128)(2,1)} %param.26) | copy-start | bytes 393220
  76.8 2.0 %copy-start.13 = (f32[128]{0:T(128)S(1)}, f32[128]{0:T(128)}, u32[]{:S(2)}) copy-start(f32[128]{0:T(128)} %param.25) | copy-start | bytes 1540

commit v5 on v4

--- a/solution.py
+++ b/solution.py
@@ -96,7 +96,7 @@
         values[first + j] = found[:, j * span : (j + 1) * span]
 
 
-def own_kernel(own, bias, gain, match, value_t, keys, part_mix, part_max, part_sum, values, scores, weights):
+def own_kernel(own, bias, gain, match, value_t, sides, part_mix, part_max, part_sum, keys, values, scores, weights):
     bins, count, width = own.shape
     depth = width // HEADS
 
@@ -108,7 +108,9 @@
     def score(u):
         for j in range(UNIT_BINS):
             b = u * UNIT_BINS + j
-            found = dot_nt(keys[b], query_sides(keys[b])) + jnp.concatenate([bias[...]] * HEADS, 1)
+            side = query_sides(keys[b])
+            sides[b] = side
+            found = dot_nt(keys[b], side) + jnp.concatenate([bias[...]] * HEADS, 1)
             scores[j] = found
             part_max[b] = jnp.max(found, 0, keepdims=True)
 
@@ -146,7 +148,7 @@
     def score(u):
         for j in range(UNIT_BINS):
             b = u * UNIT_BINS + j
-            found = dot_nt(keys[b], query_sides(queries[b])) + jnp.concatenate([bias[...]] * HEADS, 1)
+            found = dot_nt(keys[b], queries[b]) + jnp.concatenate([bias[...]] * HEADS, 1)
             scores[j] = found
             largest[j] = jnp.maximum(jnp.max(found, 0, keepdims=True), part_max[b])
 
@@ -244,7 +246,7 @@
     columns = HEADS * count
     args = (spec, bias, gain, match, value_t)
     outs = [
-        jax.ShapeDtypeStruct((bins, count, width), BF16),
+        jax.ShapeDtypeStruct((bins, columns, width), BF16),
         jax.ShapeDtypeStruct((bins, width, count), F32),
         jax.ShapeDtypeStruct((bins, 1, columns), F32),
         jax.ShapeDtypeStruct((bins, 1, columns), F32),
@@ -257,6 +259,7 @@
         out_specs=[full(o) for o in outs],
         out_shape=outs,
         scratch_shapes=[
+            pltpu.VMEM((bins, count, width), BF16),
             pltpu.VMEM((bins, width, count), BF16),
             pltpu.VMEM((UNIT_BINS, count, columns), F32),
             pltpu.VMEM((UNIT_BINS, count, columns), BF16),

time: 83.7 us -> 83.4 us (level)
  no operation moved by 1% of the time
where the time goes in v5:
time: 83.4 us; the launch traced here: 83.1 us
  blocking collectives  39.2 us (47%)
  Pallas kernels  18.9 us (23%)
  starting transfers between devices  8.57 us (10%)
  waiting for transfers between devices  6.98 us (8%)
  matrix products  5.05 us (6%)
  other arithmetic  2.31 us (3%)
  local copies, waits for them, and re-layouts  1.75 us (2%)
    all_to_all x2, blocking collectives, exchange(): lax.all_to_all(array, 'freq', split_axis=0, concat_axis=0, tiled=True)  39.2 us
    pallas_call x1, Pallas kernels, halo_stage(): call(halo_kernel, 'halo_stage', 7, in_specs=[full(a) for a in args], out_...  7.26 us
    pallas_call x1, Pallas kernels, freq_stage(): call(freq_kernel, 'freq_stage', 5, in_specs=[full(rows), full(match), ful...  7.15 us
    ppermute x1, starting transfers between devices, per_device(): after = lax.ppermute(spec[:, :HALO], 'tm', down)  6.65 us
    dot_general x2, matrix products, dot_nn(): return jnp.dot(a, b, preferred_element_type=F32)  5.05 us
    ppermute x1, waiting for transfers between devices, per_device(): after = lax.ppermute(spec[:, :HALO], 'tm', down)  4.63 us
    pallas_call x1, Pallas kernels, own_stage(): call(own_kernel, 'own_stage', 8, in_specs=[full(a) for a in args], out_sp...  4.47 us
    ppermute x1, waiting for transfers between devices, per_device(): before = lax.ppermute(spec[:, count - HALO:], 'tm', up)  2.35 us
  transfers between devices with their start and end apart: 2, of which 2 were waited for; matrix products, arithmetic and copies ran while one was open for 1% of the time, Pallas kernels for 5%

profile of v5, /device:TPU:448, one launch (start us, length us, event | category | flops | bytes accessed | tf_op | source)
XLA Modules:
  0.0 83.1 jit_solution(12762364443004336348)
XLA Ops:
  0.0 0.0 copy-start
  0.0 0.0 copy-start.1
  0.0 0.0 copy-start.9
  0.0 0.0 copy-start.8
  0.0 0.0 copy-start.10
  0.0 0.0 copy-start.11
  0.0 0.0 copy-start.5
  0.1 0.0 copy-start.2
  0.1 1.4 %fusion.39 = (bf16[32,64,128]{2,1,0:T(8,128)(2,1)S(1)}, bf16[32,64,128]{2,1,0:T(8,128)(2,1)S(1)}) fusion(bf16[32,128,128]{2,1,0:T(8,128)(2,1)} %own.3), kind=kLoop, calls=%fused_computation.43 | loop fusion | bytes 2097152 | tf_op jit(solution)/shard_map/slice | solution.py:366
  1.4 1.9 %collective-permute-start = (bf16[32,64,128]{2,1,0:T(8,128)(2,1)S(1)}, bf16[32,64,128]{2,1,0:T(8,128)(2,1)S(1)}, u32[]{:S(2)}, u32[]{:S(2)}) collective-permute-start(bf16[32,64,128]{2,1,0:T(8,128)(2,1)S(1)} %get-tuple-element.26), channel_id=1, source_target_pairs={{0,8},{8,16},{16,24},{24,32},{32,40},{40,48},{48,56},{56,64},{64,7... | collective-permute-start | bytes 1572872 | tf_op jit(solution)/shard_map/ppermute | solution.py:365
  3.4 6.7 %collective-permute-start.1 = (bf16[32,64,128]{2,1,0:T(8,128)(2,1)S(1)}, bf16[32,64,128]{2,1,0:T(8,128)(2,1)S(1)}, u32[]{:S(2)}, u32[]{:S(2)}) collective-permute-start(bf16[32,64,128]{2,1,0:T(8,128)(2,1)S(1)} %get-tuple-element.25), channel_id=1, source_target_pairs={{8,0},{16,8},{24,16},{32,24},{40,32},{48,40},{56,48},{64,56},{72,6... | collective-permute-start | bytes 1572872 | tf_op jit(solution)/shard_map/ppermute | solution.py:366
  10.0 0.0 copy-done.9
  10.0 0.1 pad_dynamic-slice_fusion.1
  10.1 0.0 copy-done.8
  10.1 0.1 compare_and_fusion
  10.2 0.1 dynamic_slice.9
  10.3 0.2 and_select_fusion
  10.5 0.0 copy-done.10
  10.5 0.1 copy.15
  10.7 0.0 copy-done.11
  10.7 0.1 copy.16
  10.8 0.0 copy-done.1
  10.8 0.0 copy-done.5
  10.8 0.0 copy-done.2
  10.8 0.0 copy-start.3
  10.8 0.0 copy-start.6
  10.9 4.5 %own_stage.1 = (bf16[32,512,128]{2,1,0:T(8,128)(2,1)S(1)}, f32[32,128,128]{2,1,0:T(8,128)S(1)}, f32[32,1,512]{2,1,0:T(1,128)S(1)}, f32[32,1,512]{2,1,0:T(1,128)S(1)}) custom-call(bf16[32,128,128]{2,1,0:T(8,128)(2,1)S(1)} %copy-done.1, f32[128,128]{1,0:T(8,128)S(1)} %slice.22.bias, f32[1,128]{1,0:T(1,128)S(1)} %bitcast.21, bf16[128,128]{1,0:T(8,128)(2,1)S(1)} %copy-done.2, ...), custom_call_target="tpu_custom_call" | custom-call | flops 4000000000 | bytes 1048576 | tf_op jit(solution)/shard_map/own_stage/pallas_call | solution.py:254
  15.3 2.4 %collective-permute-done.before = bf16[32,64,128]{2,1,0:T(8,128)(2,1)S(1)} collective-permute-done((bf16[32,64,128]{2,1,0:T(8,128)(2,1)S(1)}, bf16[32,64,128]{2,1,0:T(8,128)(2,1)S(1)}, u32[]{:S(2)}, u32[]{:S(2)}) %collective-permute-start) | collective-permute-done | bytes 524320 | tf_op jit(solution)/shard_map/ppermute | solution.py:365
  17.7 4.6 %collective-permute-done.1.after = bf16[32,64,128]{2,1,0:T(8,128)(2,1)S(1)} collective-permute-done((bf16[32,64,128]{2,1,0:T(8,128)(2,1)S(1)}, bf16[32,64,128]{2,1,0:T(8,128)(2,1)S(1)}, u32[]{:S(2)}, u32[]{:S(2)}) %collective-permute-start.1) | collective-permute-done | bytes 524320 | tf_op jit(solution)/shard_map/ppermute | solution.py:366
  22.3 0.0 copy-done.3
  22.3 0.0 copy-done.6
  22.3 7.3 %halo_stage.1 = (bf16[32,128,128]{2,1,0:T(8,128)(2,1)S(1)}, bf16[8,16,32,128]{3,2,1,0:T(8,128)(2,1)S(1)}) custom-call(bf16[32,64,128]{2,1,0:T(8,128)(2,1)S(1)} %collective-permute-done.before, bf16[32,128,128]{2,1,0:T(8,128)(2,1)S(1)} %copy-done.1, bf16[32,64,128]{2,1,0:T(8,128)(2,1)S(1)} %collective-permute-done.1.after, ...), custom_call_target="tpu_custom_call" | custom-call | flops 3500000000 | bytes 1048576 | tf_op jit(solution)/shard_map/halo_stage/pallas_call | solution.py:277
  29.6 0.0 copy-start.4
  29.6 20.5 %all_to_all.10.rows = bf16[8,16,32,128]{3,2,1,0:T(8,128)(2,1)S(1)} all-to-all(bf16[8,16,32,128]{3,2,1,0:T(8,128)(2,1)S(1)} %get-tuple-element.21), channel_id=1, replica_groups=mesh['tm'=64,'freq'=8] {'freq'}, dimensions={0} | all-to-all | bytes 2097152 | tf_op jit(solution)/shard_map/all_to_all | solution.py:385
  50.1 0.0 copy-done.4
  50.1 7.1 %freq_stage.1 = bf16[8,16,32,128]{3,2,1,0:T(8,128)(2,1)S(1)} custom-call(bf16[8,16,32,128]{3,2,1,0:T(8,128)(2,1)S(1)} %all_to_all.10.rows, bf16[128,128]{1,0:T(8,128)(2,1)S(1)} %copy-done.4, bf16[128,128]{1,0:T(8,128)(2,1)S(1)} %bitcast.18), custom_call_target="tpu_custom_call" | custom-call | flops 2500000000 | bytes 1048576 | tf_op jit(solution)/shard_map/freq_stage/pallas_call | solution.py:300
  57.2 0.0 copy-start.7
  57.2 18.8 %all_to_all.11 = bf16[8,16,32,128]{3,2,1,0:T(8,128)(2,1)S(1)} all-to-all(bf16[8,16,32,128]{3,2,1,0:T(8,128)(2,1)S(1)} %freq_stage.1), channel_id=1, replica_groups=mesh['tm'=64,'freq'=8] {'freq'}, dimensions={0} | all-to-all | bytes 2097152 | tf_op jit(solution)/shard_map/all_to_all | solution.py:385
  76.0 0.0 copy-done.7
  76.0 0.5 fusion.22
  76.5 0.0 copy-start.12
  76.5 0.0 copy-start.13
  76.6 0.6 convert_reduce_fusion
  77.2 1.3 %fusion.14 = f32[128,32]{0,1:T(8,128)S(1)} fusion(bf16[128,32,128]{2,0,1:T(8,128)(2,1)S(1)} %get-tuple-element.24, f32[128,32]{0,1:T(8,128)S(1)} %broadcast_multiply_fusion), kind=kLoop, calls=%fused_computation.16 | loop fusion | flops 2093056 | bytes 1081344 | tf_op jit(solution)/shard_map/reduce_sum | solution.py:24
  78.5 0.0 copy-done
  78.5 0.0 copy-done.12
  78.5 0.0 copy-done.13
  78.5 4.5 %fusion.17 = bf16[128,32,128]{2,0,1:T(8,128)(2,1)} fusion(bf16[128,32,128]{2,0,1:T(8,128)(2,1)S(1)} %get-tuple-element.24, f32[128]{0:T(128)S(1)} %copy-done.13, f32[128,32]{0,1:T(8,128)S(1)} %add_rsqrt_fusion, f32[128,32]{0,1:T(8,128)S(1)} %broadcast_multiply_fusion, bf16[512,128]{1,0:T(8,128)(2,1)S(1)} %copy-done, bf16[128,512]{1,0:T(8,128)(2,1)S(1)} %copy-done.12), kind=kOutput, calls=%fused_computation.19 | convolution fusion | flops 1096810496 | bytes 2392576 | tf_op jit(solution)/shard_map/dot_general | solution.py:37
  (6 shorter events, 0.0 us)
Async XLA Ops:
  0.0 78.5 %copy-start = (bf16[512,128]{1,0:T(8,128)(2,1)S(1)}, bf16[512,128]{1,0:T(8,128)(2,1)}, u32[]{:S(2)}) copy-start(bf16[512,128]{1,0:T(8,128)(2,1)} %param.27) | copy-start | bytes 393220
  0.0 10.8 %copy-start.1 = (bf16[32,128,128]{2,1,0:T(8,128)(2,1)S(1)}, bf16[32,128,128]{2,1,0:T(8,128)(2,1)}, u32[]{:S(2)}) copy-start(bf16[32,128,128]{2,1,0:T(8,128)(2,1)} %own.3) | copy-start | bytes 3145732
  0.0 10.0 %copy-start.9 = (s32[8192]{0:T(1024)S(1)}, s32[8192]{0:T(1024)}, u32[]{:S(2)}) copy-start(s32[8192]{0:T(1024)} %param.15) | copy-start | bytes 98308
  0.0 10.1 %copy-start.8 = (s32[8192]{0:T(1024)S(1)}, s32[8192]{0:T(1024)}, u32[]{:S(2)}) copy-start(s32[8192]{0:T(1024)} %param.16) | copy-start | bytes 98308
  0.0 10.5 %copy-start.10 = (bf16[128,128]{1,0:T(8,128)(2,1)S(1)}, bf16[128,128]{1,0:T(8,128)(2,1)}, u32[]{:S(2)}) copy-start(bf16[128,128]{1,0:T(8,128)(2,1)} %param.19) | copy-start | bytes 98308
  0.0 10.6 %copy-start.11 = (bf16[128,128]{1,0:T(8,128)(2,1)S(1)}, bf16[128,128]{1,0:T(8,128)(2,1)}, u32[]{:S(2)}) copy-start(bf16[128,128]{1,0:T(8,128)(2,1)} %param.23) | copy-start | bytes 98308
  0.0 10.8 %copy-start.5 = (f32[128]{0:T(128)S(1)}, f32[128]{0:T(128)}, u32[]{:S(2)}) copy-start(f32[128]{0:T(128)} %param.17) | copy-start | bytes 1540
  0.1 10.8 %copy-start.2 = (bf16[128,128]{1,0:T(8,128)(2,1)S(1)}, bf16[128,128]{1,0:T(8,128)(2,1)}, u32[]{:S(2)}) copy-start(bf16[128,128]{1,0:T(8,128)(2,1)} %match.4) | copy-start | bytes 98308
  1.4 16.3 %collective-permute-start = (bf16[32,64,128]{2,1,0:T(8,128)(2,1)S(1)}, bf16[32,64,128]{2,1,0:T(8,128)(2,1)S(1)}, u32[]{:S(2)}, u32[]{:S(2)}) collective-permute-start(bf16[32,64,128]{2,1,0:T(8,128)(2,1)S(1)} %get-tuple-element.26), channel_id=1, source_target_pairs={{0,8},{8,16},{16,24},{24,32},{32,40},{40,48},{48,56},{56,64},{64,7... | collective-permute-start | bytes 1572872 | tf_op jit(solution)/shard_map/ppermute | solution.py:365
  3.4 19.0 %collective-permute-start.1 = (bf16[32,64,128]{2,1,0:T(8,128)(2,1)S(1)}, bf16[32,64,128]{2,1,0:T(8,128)(2,1)S(1)}, u32[]{:S(2)}, u32[]{:S(2)}) collective-permute-start(bf16[32,64,128]{2,1,0:T(8,128)(2,1)S(1)} %get-tuple-element.25), channel_id=1, source_target_pairs={{8,0},{16,8},{24,16},{32,24},{40,32},{48,40},{56,48},{64,56},{72,6... | collective-permute-start | bytes 1572872 | tf_op jit(solution)/shard_map/ppermute | solution.py:366
  10.8 11.5 %copy-start.3 = (bf16[128,128]{1,0:T(8,128)(2,1)S(1)}, bf16[128,128]{1,0:T(8,128)(2,1)}, u32[]{:S(2)}) copy-start(bf16[128,128]{1,0:T(8,128)(2,1)} %out_w.1) | copy-start | bytes 98308
  10.8 11.5 %copy-start.6 = (f32[128]{0:T(128)S(1)}, f32[128]{0:T(128)}, u32[]{:S(2)}) copy-start(f32[128]{0:T(128)} %param.21) | copy-start | bytes 1540
  29.6 20.5 %copy-start.4 = (bf16[128,128]{1,0:T(8,128)(2,1)S(1)}, bf16[128,128]{1,0:T(8,128)(2,1)}, u32[]{:S(2)}) copy-start(bf16[128,128]{1,0:T(8,128)(2,1)} %match.5) | copy-start | bytes 98308
  57.2 18.8 %copy-start.7 = (bf16[128,128]{1,0:T(8,128)(2,1)S(1)}, bf16[128,128]{1,0:T(8,128)(2,1)}, u32[]{:S(2)}) copy-start(bf16[128,128]{1,0:T(8,128)(2,1)} %param.24) | copy-start | bytes 98308
  76.5 2.0 %copy-start.12 = (bf16[128,512]{1,0:T(8,128)(2,1)S(1)}, bf16[128,512]{1,0:T(8,128)(2,1)}, u32[]{:S(2)}) copy-start(bf16[128,512]{1,0:T(8,128)(2,1)} %param.26) | copy-start | bytes 393220
  76.5 2.0 %copy-start.13 = (f32[128]{0:T(128)S(1)}, f32[128]{0:T(128)}, u32[]{:S(2)}) copy-start(f32[128]{0:T(128)} %param.25) | copy-start | bytes 1540
